TPU v7x, 32 devices: a whole 2x2x4 slice. The times are simulated.
32 devices in a mesh: tm: 8 (over z, x), rows: 4 (over y, core).
Axes of the slice: x: 2, y: 2, z: 4, core: 2. Of those that a mesh axis runs over, the one named last changes fastest.
Arguments:
- frames: bfloat16 [8, 32, 64, 128], P('tm', 'rows'), may hold values from -6 to 6
- decays: float32 [8, 256], P('tm'), may hold values from 0.4 to 1
- in_weight: bfloat16 [3, 3, 128, 256], replicated, may hold values from -0.046875 to 0.046875
- out_weight: bfloat16 [3, 3, 256, 128], replicated, may hold values from -0.125 to 0.125
- skip_gain: float32 [128], replicated, may hold values from 0.25 to 1.75
- cotangent: bfloat16 [8, 32, 64, 128], P('tm', 'rows'), may hold values from -6 to 6
Outputs:
- output_frames: bfloat16 [8, 32, 64, 128], P('tm', 'rows')
- input_grad: bfloat16 [8, 32, 64, 128], P('tm', 'rows')
- in_weight_grad: float32 [3, 3, 128, 256], replicated
- out_weight_grad: float32 [3, 3, 256, 128], replicated
- gain_grad: float32 [128], replicated
- decay_grad: float32 [8, 256], P('tm')
All inputs are finite; a program needn't handle non-finite values.
Results may differ from a plain program's by a relative error of at most 0.008.
Values may be sent and summed in bfloat16 or wider, within the bound.
A program may use at most 192 MiB of HBM per device.

v0:
```python
import math

import jax
import jax.numpy as jnp
from jax import lax
from jax.sharding import PartitionSpec as P


def padded_2(block, sides, width):
    for axis, dim in sides:
        count = lax.axis_size(axis)
        forward = [(i, i + 1) for i in range(count - 1)]
        backward = [(target, source) for source, target in forward]
        low = lax.ppermute(
            lax.slice_in_dim(block, block.shape[dim] - width, None, axis=dim), axis, forward
        )
        high = lax.ppermute(lax.slice_in_dim(block, 0, width, axis=dim), axis, backward)
        block = jnp.concatenate([low, block, high], axis=dim)
    return block


def entering(array, axis, join, neutral, backward):
    count = lax.axis_size(axis)
    place = lax.axis_index(axis)
    ahead = count - 1 - place if backward else place
    gathered = jax.tree.map(
        lambda a, kind: lax.all_gather(a.astype(kind), axis), array, (jnp.bfloat16, jnp.bfloat16)
    )
    state = jax.tree.map(lambda a, e: jnp.zeros_like(a) + jnp.asarray(e, a.dtype), array, neutral)

    def one(turn, state):
        source = count - 1 - turn if backward else turn
        return join(
            state,
            jax.tree.map(
                lambda a, own: lax.dynamic_index_in_dim(a, source, 0, False).astype(own.dtype),
                gathered,
                array,
            ),
        )

    return lax.fori_loop(0, ahead, one, state)


def pad_columns(padded_rows):
    return jnp.pad(padded_rows, ((0, 0), (0, 0), (1, 1), (0, 0)))


def conv_taps(padded, weights):
    frame_count = padded.shape[0]
    height = padded.shape[1] - 2
    across = padded.shape[2] - 2
    channels = padded.shape[3]
    result = jnp.zeros((frame_count * height * across, weights.shape[3]), jnp.float32)
    for row_tap in range(3):
        for col_tap in range(3):
            window = padded[:, row_tap : row_tap + height, col_tap : col_tap + across, :].reshape(
                -1, channels
            )
            result = result + jnp.dot(
                window, weights[row_tap, col_tap], preferred_element_type=jnp.float32
            )
    return result.reshape(frame_count, height, across, weights.shape[3])


def tap_grads(padded, grad_field):
    height = grad_field.shape[1]
    across = grad_field.shape[2]
    channels = padded.shape[3]
    flat_grad = grad_field.reshape(-1, grad_field.shape[3])
    outer_list = []
    for row_tap in range(3):
        inner_list = []
        for col_tap in range(3):
            window = padded[:, row_tap : row_tap + height, col_tap : col_tap + across, :].reshape(
                -1, channels
            )
            inner_list.append(
                lax.dot_general(
                    window, flat_grad, (((0,), (0,)), ((), ())), preferred_element_type=jnp.float32
                )
            )
        outer_list.append(jnp.stack(inner_list))
    return jnp.stack(outer_list)


def flipped(weights):
    return jnp.transpose(weights[::-1, ::-1], (0, 1, 3, 2))


def combine(earlier, later):
    return (earlier[0] * later[0], later[0][None, None, :] * earlier[1] + later[1])


def on_device(frames, decays, in_weight, out_weight, skip_gain, cotangent):
    frame_count, band_rows, across, channels = frames.shape
    states_width = in_weight.shape[3]
    total_frames = frame_count * lax.axis_size("tm")
    total_rows = band_rows * lax.axis_size("rows")
    cell_norm = 1.0 / math.sqrt(total_frames * total_rows * across)
    frame_norm = 1.0 / math.sqrt(total_rows * across)
    in_pad = pad_columns(padded_2(frames, (("rows", 1),), 1))
    drive_terms = conv_taps(in_pad, in_weight)

    def forward_step(state, inputs):
        decay_now, drive_now = inputs
        state = decay_now[None, None, :] * state + drive_now
        return (state, state)

    zero_state = jnp.zeros((band_rows, across, states_width), jnp.float32)
    _, local_states = lax.scan(forward_step, zero_state, (decays, drive_terms))
    decay_prefix = jnp.cumprod(decays, axis=0)
    identity = (jnp.ones((states_width,), jnp.float32), zero_state)
    carried = entering((decay_prefix[-1], local_states[-1]), "tm", combine, identity, False)[1]
    states = local_states + decay_prefix[:, None, None, :] * carried[None]
    rounded = states.astype(jnp.bfloat16)
    state_pad = pad_columns(padded_2(rounded, (("rows", 1),), 1))
    output_frames = (
        conv_taps(state_pad, out_weight) + skip_gain * frames.astype(jnp.float32)
    ).astype(jnp.bfloat16)
    cot_pad = pad_columns(padded_2(cotangent, (("rows", 1),), 1))
    from_output = conv_taps(cot_pad, flipped(out_weight))
    next_decay = jnp.concatenate([decays[1:], jnp.zeros((1, states_width), jnp.float32)], axis=0)

    def backward_step(adjoint_now, inputs):
        decay_next, from_now = inputs
        adjoint_now = from_now + decay_next[None, None, :] * adjoint_now
        return (adjoint_now, adjoint_now)

    _, local_adjoint = lax.scan(backward_step, zero_state, (next_decay, from_output), reverse=True)
    later_decay = jnp.concatenate([decays[1:], jnp.ones((1, states_width), jnp.float32)], axis=0)
    decay_suffix = jnp.cumprod(later_decay[::-1], axis=0)[::-1]
    leading = decays[0][None, None, :] * local_adjoint[0]
    incoming = entering((decay_prefix[-1], leading), "tm", combine, identity, True)[1]
    adjoint = local_adjoint + decay_suffix[:, None, None, :] * incoming[None]
    previous = jnp.concatenate([carried[None], states[:-1]], axis=0)
    decay_terms = jnp.sum(adjoint * previous, axis=(1, 2)) * frame_norm
    adjoint_low = adjoint.astype(jnp.bfloat16)
    in_grad_terms = tap_grads(in_pad, adjoint_low) * cell_norm
    out_grad_terms = tap_grads(state_pad, cotangent) * cell_norm
    gain_terms = (
        jnp.sum(cotangent.astype(jnp.float32) * frames.astype(jnp.float32), axis=(0, 1, 2))
        * cell_norm
    )
    adjoint_pad = pad_columns(padded_2(adjoint_low, (("rows", 1),), 1))
    input_grad = (
        conv_taps(adjoint_pad, flipped(in_weight)) + skip_gain * cotangent.astype(jnp.float32)
    ).astype(jnp.bfloat16)
    in_weight_grad, out_weight_grad, gain_grad = lax.psum(
        (in_grad_terms, out_grad_terms, gain_terms), ("tm", "rows")
    )
    decay_grad = lax.psum(decay_terms, "rows")
    return (output_frames, input_grad, in_weight_grad, out_weight_grad, gain_grad, decay_grad)


def solution(mesh):
    in_specs = (
        P("tm", "rows", None, None),
        P("tm", None),
        P(),
        P(),
        P(),
        P("tm", "rows", None, None),
    )
    out_specs = (
        P("tm", "rows", None, None),
        P("tm", "rows", None, None),
        P(),
        P(),
        P(),
        P("tm", None),
    )
    return jax.shard_map(
        on_device, mesh=mesh, in_specs=in_specs, out_specs=out_specs, check_vma=False
    )
```

profile of v0, /device:TPU:0, one launch (start us, length us, event | category | flops | bytes accessed | tf_op | source)
XLA Modules:
  0.0 304.3 jit_solution(4210442601135215782)
XLA Ops:
  7.2 0.8 fusion.102
  8.0 1.3 collective-permute-start.1
  9.3 3.0 collective-permute-start
  12.3 0.7 broadcast_multiply_fusion.1
  13.2 1.0 select_maximum_fusion.6
  14.7 0.3 copy-done.1
  16.6 0.7 add_convert_fusion.1
  17.4 1.3 collective-permute-start.5
  18.8 5.1 %collective-permute-start.4 = (bf16[1,1,64,128]{3,2,1,0:T(8,128)(2,1)S(1)}, bf16[1,1,64,128]{3,2,1,0:T(8,128)(2,1)S(1)}, u32[]{:S(2)}, u32[]{:S(2)}) collective-permute-start(bf16[1,1,64,128]{3,2,1,0:T(8,128)(2,1)S(1)} %get-tuple-element.225), channel_id=1, source_target_pairs={{0,1},{1,2},{2,3},{4,5},{5,6},{6,7},{8,9},{9,10},{10,11},{12,13},{... | collective-permute-start | bytes 49160 | tf_op jit(solution)/shard_map/ppermute | solution.py:14
  24.0 0.8 collective-permute-done.4
  25.0 0.2 fusion.41
  25.4 0.2 convolution_add_fusion.6
  25.7 0.2 convolution_add_fusion.5
  25.9 0.2 convolution_add_fusion.4
  26.1 0.2 convolution_add_fusion.3
  26.4 0.2 convolution_add_fusion.2
  26.6 0.2 convolution_add_fusion.1
  27.1 0.4 copy-done.9
  27.5 0.8 multiply_convert_fusion
  28.4 20.8 %all-gather = bf16[8,1,256]{2,1,0:T(2,128)(2,1)S(1)} all-gather(bf16[1,1,256]{2,1,0:T(2,128)(2,1)S(1)} %convert_bitcast_fusion), channel_id=1, replica_groups=mesh['tm'=8,'rows'=4] {'tm'}, dimensions={0}, use_global_device_ids=true | all-gather | bytes 4608 | tf_op jit(solution)/shard_map/all_gather | solution.py:27
  49.2 0.9 reverse_bitcast_fusion
  50.1 21.5 %all-gather.4.cloned.1.call-done = bf16[8,8,64,256]{3,2,1,0:T(8,128)(2,1)} async-done(((bf16[1,8,64,256]{3,2,1,0:T(8,128)(2,1)}), bf16[8,8,64,256]{3,2,1,0:T(8,128)(2,1)}) %all-gather.4.cloned.1.call-update) | async-done | bytes 2097168 | tf_op jit(solution)/shard_map/all_gather | solution.py:27
  71.6 49.9 %all-gather.6.cloned.1.call-done = bf16[8,8,64,256]{3,2,1,0:T(8,128)(2,1)} async-done(((bf16[1,8,64,256]{3,2,1,0:T(8,128)(2,1)}), bf16[8,8,64,256]{3,2,1,0:T(8,128)(2,1)}) %all-gather.6.cloned.1.call-update) | async-done | bytes 2097168 | tf_op jit(solution)/shard_map/all_gather | solution.py:27
  121.5 8.5 %while.17 = (s32[]{:T(128)}, f32[8,64,256]{2,1,0:T(8,128)S(1)}, s32[]{:T(128)}, bf16[8,256]{1,0:T(8,128)(2,1)S(1)}, bf16[8,8,64,256]{3,2,1,0:T(8,128)(2,1)}, /*index=5*/s32[]{:T(128)}, s32[]{:T(128)}, s32[]{:T(128)}, s32[]{:T(128)}) while((s32[]{:T(128)}, f32[8,64,256]{2,1,0:T(8,128)S(1)}, s32[]{:T(128)}, bf16[8,256]{1,0:T(8,128)(2,1)S(1)}, ...), condition=%wide.region_4.5_spmd, body=%wide.region_3.4_spmd.sunk | while | flops 393478 | bytes 1313435 | solution.py:42
  121.6 1.2 convert_add_fusion.5
  122.8 1.2 convert_add_fusion.5
  124.0 1.2 convert_add_fusion.5
  125.2 1.2 convert_add_fusion.5
  126.4 1.2 convert_add_fusion.5
  127.6 1.2 convert_add_fusion.5
  128.9 1.2 convert_add_fusion.5
  130.3 0.2 convolution_bitcast_fusion.15
  130.9 0.2 convolution_bitcast_fusion.9
  131.4 0.2 convolution_bitcast_fusion.11
  131.9 0.2 convolution_bitcast_fusion.13
  132.4 1.3 collective-permute-start.7
  133.7 3.0 collective-permute-start.6
  136.7 0.3 convolution_bitcast_fusion.4
  137.0 1.3 collective-permute-start.3
  138.3 3.6 %collective-permute-start.2 = (bf16[1,1,64,256]{3,2,1,0:T(8,128)(2,1)S(1)}, bf16[1,1,64,256]{3,2,1,0:T(8,128)(2,1)S(1)}, u32[]{:S(2)}, u32[]{:S(2)}) collective-permute-start(bf16[1,1,64,256]{3,2,1,0:T(8,128)(2,1)S(1)} %get-tuple-element.206), channel_id=1, source_target_pairs={{0,1},{1,2},{2,3},{4,5},{5,6},{6,7},{8,9},{9,10},{10,11},{12,13},{... | collective-permute-start | bytes 98312 | tf_op jit(solution)/shard_map/ppermute | solution.py:14
  142.0 1.1 maximum_multiply_fusion
  143.2 7.9 %psum.31 = f32[1,256]{1,0:T(1,128)} all-reduce(f32[1,256]{1,0:T(1,128)S(1)} %bitcast.421), channel_id=1, replica_groups=mesh['tm'=8,'rows'=4] {'rows'}, use_global_device_ids=true, to_apply=%region_10.11 | all-reduce | flops 256 | bytes 2048 | tf_op jit(solution)/shard_map/psum | solution.py:152
  151.4 0.3 convolution_bitcast_fusion
  151.7 0.3 convolution_bitcast_fusion.2
  151.9 0.3 convolution_bitcast_fusion.6
  152.2 0.3 convolution_bitcast_fusion.8
  152.5 0.3 convolution_bitcast_fusion.3
  152.7 0.3 convolution_bitcast_fusion.5
  153.4 0.8 copy-done.5
  154.9 0.3 convolution_bitcast_fusion.1
  155.2 0.3 convolution_bitcast_fusion.7
  155.5 0.2 convolution_add_fusion.20
  155.8 0.2 convolution_add_fusion.19
  156.5 0.2 convolution_add_fusion.16
  156.7 0.9 convolution_add_fusion.15
  158.6 0.2 convolution_add_fusion.23
  158.8 1.0 convolution_add_fusion.22
  159.8 1.1 maximum_multiply_fusion.1
  161.2 0.7 copy-done.7
  162.4 0.8 fusion.11
  163.2 37.1 %psum.30 = f32[128]{0:T(128)} all-reduce(f32[128]{0:T(128)S(1)} %broadcast_multiply_fusion.2), channel_id=1, replica_groups=mesh['tm'=8,'rows'=4] {'tm','rows'}, use_global_device_ids=true, to_apply=%region_8.9 | all-reduce | flops 128 | bytes 1024 | tf_op jit(solution)/shard_map/psum | solution.py:149
  200.3 94.0 %all-reduce.7.cloned.1.call-done = (f32[3,3,128,256]{3,2,1,0:T(8,128)}, f32[3,3,256,128]{3,2,1,0:T(8,128)}) async-done(((f32[3,3,128,256]{3,2,1,0:T(8,128)}, f32[3,3,256,128]{3,2,1,0:T(8,128)}), (f32[3,3,128,256]{3,2,1,0:T(8,128)}, f32[3,3,256,128]{3,2,1,0:T(8,128)})) %all-reduce.7.cloned.1.call-update) | async-done | bytes 2359312 | tf_op jit(solution)/shard_map/psum | solution.py:149
  294.3 2.5 copy.34
  296.8 1.0 copy.35
  (94 shorter events, 8.2 us)
Async XLA Ops:
  7.2 7.1 %copy-start.2 = (bf16[3,3,128,256]{3,2,1,0:T(8,128)(2,1)S(1)}, bf16[3,3,128,256]{3,2,1,0:T(8,128)(2,1)}, u32[]{:S(2)}) copy-start(bf16[3,3,128,256]{3,2,1,0:T(8,128)(2,1)} %param.12) | copy-start | bytes 1769476
  7.2 64.4 %all-gather.4.cloned.1.call-start = ((), (), s32[]{:S(2)}) async-start(), calls=%async_computation | async-start | bytes 2359296 | tf_op jit(solution)/shard_map/all_gather | solution.py:27
  8.0 5.0 %collective-permute-start.1 = (bf16[1,1,64,128]{3,2,1,0:T(8,128)(2,1)S(1)}, bf16[1,1,64,128]{3,2,1,0:T(8,128)(2,1)S(1)}, u32[]{:S(2)}, u32[]{:S(2)}) collective-permute-start(bf16[1,1,64,128]{3,2,1,0:T(8,128)(2,1)S(1)} %get-tuple-element.230), channel_id=1, source_target_pairs={{1,0},{2,1},{3,2},{5,4},{6,5},{7,6},{9,8},{10,9},{11,10},{13,12},{... | collective-permute-start | bytes 49160 | tf_op jit(solution)/shard_map/ppermute | solution.py:17
  9.3 3.9 %collective-permute-start = (bf16[1,1,64,128]{3,2,1,0:T(8,128)(2,1)S(1)}, bf16[1,1,64,128]{3,2,1,0:T(8,128)(2,1)S(1)}, u32[]{:S(2)}, u32[]{:S(2)}) collective-permute-start(bf16[1,1,64,128]{3,2,1,0:T(8,128)(2,1)S(1)} %get-tuple-element.229), channel_id=1, source_target_pairs={{0,1},{1,2},{2,3},{4,5},{5,6},{6,7},{8,9},{9,10},{10,11},{12,13},{... | collective-permute-start | bytes 49160 | tf_op jit(solution)/shard_map/ppermute | solution.py:14
  14.1 0.9 copy-start.1
  16.4 1.1 copy-start
  16.4 7.5 %copy-start.3 = (bf16[3,3,256,128]{3,2,1,0:T(8,128)(2,1)S(1)}, bf16[3,3,256,128]{3,2,1,0:T(8,128)(2,1)}, u32[]{:S(2)}) copy-start(bf16[3,3,256,128]{3,2,1,0:T(8,128)(2,1)} %param.13) | copy-start | bytes 1769476
  17.4 104.1 %all-gather.6.cloned.1.call-start = ((), (), s32[]{:S(2)}) async-start(), calls=%async_computation.1 | async-start | bytes 2359296 | tf_op jit(solution)/shard_map/all_gather | solution.py:27
  17.4 6.5 %collective-permute-start.5 = (bf16[1,1,64,128]{3,2,1,0:T(8,128)(2,1)S(1)}, bf16[1,1,64,128]{3,2,1,0:T(8,128)(2,1)S(1)}, u32[]{:S(2)}, u32[]{:S(2)}) collective-permute-start(bf16[1,1,64,128]{3,2,1,0:T(8,128)(2,1)S(1)} %get-tuple-element.226), channel_id=1, source_target_pairs={{1,0},{2,1},{3,2},{5,4},{6,5},{7,6},{9,8},{10,9},{11,10},{13,12},{... | collective-permute-start | bytes 49160 | tf_op jit(solution)/shard_map/ppermute | solution.py:17
  18.8 6.0 %collective-permute-start.4 = (bf16[1,1,64,128]{3,2,1,0:T(8,128)(2,1)S(1)}, bf16[1,1,64,128]{3,2,1,0:T(8,128)(2,1)S(1)}, u32[]{:S(2)}, u32[]{:S(2)}) collective-permute-start(bf16[1,1,64,128]{3,2,1,0:T(8,128)(2,1)S(1)} %get-tuple-element.225), channel_id=1, source_target_pairs={{0,1},{1,2},{2,3},{4,5},{5,6},{6,7},{8,9},{9,10},{10,11},{12,13},{... | collective-permute-start | bytes 49160 | tf_op jit(solution)/shard_map/ppermute | solution.py:14
  26.8 0.7 copy-start.9
  28.3 266.0 %all-reduce.7.cloned.1.call-start = ((), (), s32[]{:S(2)}) async-start(), calls=%async_computation.2 | async-start | bytes 4718592 | tf_op jit(solution)/shard_map/psum | solution.py:149
  132.4 20.7 %collective-permute-start.7 = (bf16[1,1,64,256]{3,2,1,0:T(8,128)(2,1)S(1)}, bf16[1,1,64,256]{3,2,1,0:T(8,128)(2,1)S(1)}, u32[]{:S(2)}, u32[]{:S(2)}) collective-permute-start(bf16[1,1,64,256]{3,2,1,0:T(8,128)(2,1)S(1)} %get-tuple-element.203), channel_id=1, source_target_pairs={{1,0},{2,1},{3,2},{5,4},{6,5},{7,6},{9,8},{10,9},{11,10},{13,12},{... | collective-permute-start | bytes 98312 | tf_op jit(solution)/shard_map/ppermute | solution.py:17
  133.7 19.4 %collective-permute-start.6 = (bf16[1,1,64,256]{3,2,1,0:T(8,128)(2,1)S(1)}, bf16[1,1,64,256]{3,2,1,0:T(8,128)(2,1)S(1)}, u32[]{:S(2)}, u32[]{:S(2)}) collective-permute-start(bf16[1,1,64,256]{3,2,1,0:T(8,128)(2,1)S(1)} %get-tuple-element.202), channel_id=1, source_target_pairs={{0,1},{1,2},{2,3},{4,5},{5,6},{6,7},{8,9},{9,10},{10,11},{12,13},{... | collective-permute-start | bytes 98312 | tf_op jit(solution)/shard_map/ppermute | solution.py:14
  137.0 14.1 %collective-permute-start.3 = (bf16[1,1,64,256]{3,2,1,0:T(8,128)(2,1)S(1)}, bf16[1,1,64,256]{3,2,1,0:T(8,128)(2,1)S(1)}, u32[]{:S(2)}, u32[]{:S(2)}) collective-permute-start(bf16[1,1,64,256]{3,2,1,0:T(8,128)(2,1)S(1)} %get-tuple-element.207), channel_id=1, source_target_pairs={{1,0},{2,1},{3,2},{5,4},{6,5},{7,6},{9,8},{10,9},{11,10},{13,12},{... | collective-permute-start | bytes 98312 | tf_op jit(solution)/shard_map/ppermute | solution.py:17
  138.3 12.8 %collective-permute-start.2 = (bf16[1,1,64,256]{3,2,1,0:T(8,128)(2,1)S(1)}, bf16[1,1,64,256]{3,2,1,0:T(8,128)(2,1)S(1)}, u32[]{:S(2)}, u32[]{:S(2)}) collective-permute-start(bf16[1,1,64,256]{3,2,1,0:T(8,128)(2,1)S(1)} %get-tuple-element.206), channel_id=1, source_target_pairs={{0,1},{1,2},{2,3},{4,5},{5,6},{6,7},{8,9},{9,10},{10,11},{12,13},{... | collective-permute-start | bytes 98312 | tf_op jit(solution)/shard_map/ppermute | solution.py:14
  153.1 1.1 copy-start.5
  153.4 1.3 copy-start.4
  161.0 0.9 copy-start.7
  161.0 1.2 copy-start.8
  161.2 1.2 copy-start.10
  294.3 2.5 copy-start.6
Sparse Core Ops, SparseCore 0:
  17.5 53.9 all-gather.3
  73.7 47.7 all-gather.5
  161.1 133.1 all-reduce.6
where the time goes:
time: 305 us; the launch traced here: 304 us
  waiting for transfers between devices  166 us (54%)
  blocking collectives  65.8 us (22%)
  starting transfers between devices  20.1 us (7%)
  other arithmetic  15.3 us (5%)
  between operations  14.4 us (5%)
  matrix products  13.9 us (5%)
  local copies, waits for them, and re-layouts  8.25 us (3%)
    psum x1, waiting for transfers between devices, on_device(): lax.psum((in_grad_terms, out_grad_terms, gain_terms), ('tm', 'rows'))  94 us
    all_gather x2, waiting for transfers between devices, entering(): lax.all_gather(a.astype(kind), axis)  71.4 us
    psum x1, blocking collectives, on_device(): lax.psum((in_grad_terms, out_grad_terms, gain_terms), ('tm', 'rows'))  37.1 us
    all_gather x1, blocking collectives, entering(): lax.all_gather(a.astype(kind), axis)  20.8 us
    ppermute x4, starting transfers between devices, padded_2(): lax.ppermute(lax.slice_in_dim(block, block.shape[dim] - width, None, axis...  14.8 us
    dot_general x36, matrix products, conv_taps(): jnp.dot(window, weights[row_tap, col_tap], preferred_element_type=jnp.flo...  9.44 us
    add x7, other arithmetic, combine(): later[0][None, None, :] * earlier[1] + later[1]  8.23 us
    psum x1, blocking collectives, on_device(): decay_grad = lax.psum(decay_terms, 'rows')  7.91 us
  transfers between devices with their start and end apart: 11, of which 5 were waited for; matrix products, arithmetic and copies ran while one was open for 3% of the time, Pallas kernels for 0%

commit v1 on v0

v1 whole, which is shorter than its diff:
```python
import functools
import math

import jax
import jax.numpy as jnp
from jax import lax
from jax.experimental import pallas as pl
from jax.experimental.pallas import tpu as pltpu
from jax.sharding import PartitionSpec as P

F32 = jnp.float32
BF16 = jnp.bfloat16
MESH = pl.DeviceIdType.MESH


def dot_nn(a, b):
    return lax.dot_general(a, b, (((1,), (0,)), ((), ())), preferred_element_type=F32)


def dot_nt(a, b):
    return lax.dot_general(a, b, (((1,), (1,)), ((), ())), preferred_element_type=F32)


def dot_tn(a, b):
    return lax.dot_general(a, b, (((0,), (0,)), ((), ())), preferred_element_type=F32)


def put_shifted(cat, first, value, across):
    cells, width = value.shape
    rows = cells // across
    wide = value.astype(F32)
    column = lax.broadcasted_iota(jnp.int32, (rows, across, width), 1)
    left = pltpu.roll(wide, 1, 0).reshape(rows, across, width)
    right = pltpu.roll(wide, cells - 1, 0).reshape(rows, across, width)
    cat[first : first + rows, :, 0:width] = jnp.where(column == 0, 0.0, left).astype(BF16)
    cat[first : first + rows, :, width : 2 * width] = value.reshape(rows, across, width)
    cat[first : first + rows, :, 2 * width : 3 * width] = jnp.where(
        column == across - 1, 0.0, right
    ).astype(BF16)


def kernel(
    n_tm, n_rows, pp, cell_norm, frame_norm,
    frames, decays, in_w, out_w, gain, cot,
    y_out, dx_out, gin_out, gout_out, ggain_out, gdec_out,
    halo_s, halo_r, dec_s, dec_all, cat_f, cat_c,
    st_d, st_o, rc_d, rc_o, st32, out_s, out_j, dp_s, dp_r, got_s, got_j,
    halo2_s, halo2_r, cat_s, cat_j,
    grads, rs_r, quarter, rs_t, piece, full, sm_s, sm_r, sm2_s, sm2_r,
    halo_ss, halo_rs, halo2_ss, halo2_rs, dec_ss, dec_rs,
    a_ss, a_rs, b_ss, b_rs, r_ss, r_rs, t_ss, t_rs, gt_ss, gt_rs, gr_ss, gr_rs,
):
    tm = lax.axis_index("tm")
    row = lax.axis_index("rows")
    _, band, across, ch = frames.shape
    s_ch = in_w.shape[3]
    cells = band * across
    chunk = cells // n_tm
    qb = n_tm * pp

    def flat(ref):
        if chunk % 16 == 0:
            return ref[...].reshape(cells, s_ch)
        return ref[...].astype(F32).reshape(cells, s_ch).astype(BF16)

    def others(axis_n, me, body):
        def one(s, carry):
            body(lax.rem(me + s, axis_n))
            return carry

        lax.fori_loop(1, axis_n, one, 0)

    def tm_copy(src, dst, ss, rs, peer):
        return pltpu.make_async_remote_copy(
            src_ref=src, dst_ref=dst, send_sem=ss, recv_sem=rs,
            device_id={"tm": peer}, device_id_type=MESH,
        )

    def row_copy(src, dst, ss, rs, peer):
        return pltpu.make_async_remote_copy(
            src_ref=src, dst_ref=dst, send_sem=ss, recv_sem=rs,
            device_id={"rows": peer}, device_id_type=MESH,
        )

    has_low = row > 0
    has_high = row < n_rows - 1

    def halo_up(s, r, ss, rs):
        return row_copy(s.at[0], r.at[1], ss.at[0], rs.at[1], row - 1)

    def halo_down(s, r, ss, rs):
        return row_copy(s.at[1], r.at[0], ss.at[1], rs.at[0], row + 1)

    def halo_start(s, r, ss, rs):
        @pl.when(has_low)
        def _():
            halo_up(s, r, ss, rs).start()

        @pl.when(has_high)
        def _():
            halo_down(s, r, ss, rs).start()

        @pl.when(jnp.logical_not(has_low))
        def _():
            r[0] = jnp.zeros(r.shape[1:], r.dtype)

        @pl.when(jnp.logical_not(has_high))
        def _():
            r[1] = jnp.zeros(r.shape[1:], r.dtype)

    def halo_wait(s, r, ss, rs):
        @pl.when(has_low)
        def _():
            row_copy(s.at[0], r.at[0], ss.at[0], rs.at[0], row - 1).wait_recv()

        @pl.when(has_high)
        def _():
            row_copy(s.at[1], r.at[1], ss.at[1], rs.at[1], row + 1).wait_recv()

    def halo_end(s, r, ss, rs):
        @pl.when(has_low)
        def _():
            halo_up(s, r, ss, rs).wait_send()

        @pl.when(has_high)
        def _():
            halo_down(s, r, ss, rs).wait_send()

    barrier = pltpu.get_barrier_semaphore()
    others(n_tm, tm, lambda p: pl.semaphore_signal(
        barrier, inc=1, device_id={"tm": p}, device_id_type=MESH))
    others(n_rows, row, lambda p: pl.semaphore_signal(
        barrier, inc=1, device_id={"rows": p}, device_id_type=MESH))
    halo_s[0, 0] = frames[0, 0]
    halo_s[0, 1] = cot[0, 0]
    halo_s[1, 0] = frames[0, band - 1]
    halo_s[1, 1] = cot[0, band - 1]
    own_decay = jnp.broadcast_to(decays[...], (8, s_ch))
    dec_s[...] = own_decay
    dec_all[tm] = own_decay
    pl.semaphore_wait(barrier, n_tm - 1 + n_rows - 1)

    halo_start(halo_s, halo_r, halo_ss, halo_rs)
    others(n_tm, tm, lambda p: tm_copy(
        dec_s, dec_all.at[tm], dec_ss.at[p], dec_rs.at[tm], p).start())

    frames_own = frames[0].reshape(cells, ch)
    cot_own = cot[0].reshape(cells, ch)
    put_shifted(cat_f, 1, frames_own, across)
    put_shifted(cat_c, 1, cot_own, across)
    gain_sum = jnp.sum(
        frames_own.astype(F32) * cot_own.astype(F32), axis=0, keepdims=True) * cell_norm
    sm_s[...] = jnp.zeros(sm_s.shape, F32)
    sm_s[1:2, 0:ch] = gain_sum

    halo_wait(halo_s, halo_r, halo_ss, halo_rs)
    put_shifted(cat_f, 0, halo_r[0, 0], across)
    put_shifted(cat_f, band + 1, halo_r[1, 0], across)
    put_shifted(cat_c, 0, halo_r[0, 1], across)
    put_shifted(cat_c, band + 1, halo_r[1, 1], across)

    acc = None
    for i in range(3):
        term = dot_nn(cat_f[i : i + band].reshape(cells, 3 * ch), in_w[i].reshape(3 * ch, s_ch))
        acc = term if acc is None else acc + term
    st_d[...] = acc.reshape(n_tm, chunk, s_ch).astype(BF16)
    others(n_tm, tm, lambda p: tm_copy(
        st_d.at[p], rc_d.at[tm], a_ss.at[0, p], a_rs.at[0, tm], p).start())
    rc_d[tm] = st_d[tm]

    acc = None
    for i in range(3):
        for j in range(3):
            window = cat_c[i : i + band, :, j * ch : (j + 1) * ch].reshape(cells, ch)
            term = dot_nt(window, out_w[2 - i, 2 - j])
            acc = term if acc is None else acc + term
    st_o[...] = acc.reshape(n_tm, chunk, s_ch).astype(BF16)
    others(n_tm, tm, lambda p: tm_copy(
        st_o.at[p], rc_o.at[tm], a_ss.at[1, p], a_rs.at[1, tm], p).start())
    rc_o[tm] = st_o[tm]

    others(n_tm, tm, lambda p: tm_copy(
        dec_s, dec_all.at[p], dec_ss.at[p], dec_rs.at[p], p).wait_recv())
    others(n_tm, tm, lambda p: tm_copy(
        st_d.at[p], rc_d.at[p], a_ss.at[0, p], a_rs.at[0, p], p).wait_recv())

    def forward(t, state):
        state = dec_all[t][0:1] * state + rc_d[t].astype(F32)
        st32[t + 1] = state
        out_s[t] = state.astype(BF16)
        return state

    st32[0] = jnp.zeros((chunk, s_ch), F32)
    lax.fori_loop(0, n_tm, forward, jnp.zeros((chunk, s_ch), F32))
    others(n_tm, tm, lambda p: tm_copy(
        out_s.at[p], got_s.at[tm], b_ss.at[0, p], b_rs.at[0, tm], p).start())
    got_s[tm] = out_s[tm]

    others(n_tm, tm, lambda p: tm_copy(
        st_o.at[p], rc_o.at[p], a_ss.at[1, p], a_rs.at[1, p], p).wait_recv())

    def backward(turn, carried):
        t = n_tm - 1 - turn
        adjoint = rc_o[t].astype(F32) + carried
        out_j[t] = adjoint.astype(BF16)
        dp_s[t] = jnp.sum((adjoint * st32[t]).reshape(chunk // 8, 8, s_ch), axis=0)
        return dec_all[t][0:1] * adjoint

    lax.fori_loop(0, n_tm, backward, jnp.zeros((chunk, s_ch), F32))
    others(n_tm, tm, lambda p: tm_copy(
        out_j.at[p], got_j.at[tm], b_ss.at[1, p], b_rs.at[1, tm], p).start())
    others(n_tm, tm, lambda p: tm_copy(
        dp_s.at[p], dp_r.at[tm], b_ss.at[2, p], b_rs.at[2, tm], p).start())
    got_j[tm] = out_j[tm]
    dp_r[tm] = dp_s[tm]

    others(n_tm, tm, lambda p: tm_copy(
        out_s.at[p], got_s.at[p], b_ss.at[0, p], b_rs.at[0, p], p).wait_recv())
    states_own = flat(got_s)
    for i in range(3):
        value = dot_tn(states_own, cat_c[i : i + band].reshape(cells, 3 * ch)) * cell_norm
        for j in range(3):
            tap = (2 - i) * 3 + 2 - j
            base = 9 * s_ch * ch // 2048 + tap * (s_ch // 16)
            grads[base : base + s_ch // 16] = (
                value[:, j * ch : (j + 1) * ch].astype(BF16).reshape(s_ch // 16, 16, ch))

    others(n_tm, tm, lambda p: tm_copy(
        out_j.at[p], got_j.at[p], b_ss.at[1, p], b_rs.at[1, p], p).wait_recv())
    adj_own = flat(got_j)
    halo2_s[0, 0] = states_own[0:across]
    halo2_s[0, 1] = adj_own[0:across]
    halo2_s[1, 0] = states_own[cells - across :]
    halo2_s[1, 1] = adj_own[cells - across :]
    halo_start(halo2_s, halo2_r, halo2_ss, halo2_rs)
    blocks = 3 * ch // 16
    for i in range(3):
        value = dot_tn(cat_f[i : i + band].reshape(cells, 3 * ch), adj_own) * cell_norm
        for h in range(s_ch // 128):
            base = (h * 3 + i) * blocks
            grads[base : base + blocks] = (
                value[:, h * 128 : (h + 1) * 128].astype(BF16).reshape(blocks, 16, 128))
    used = 18 * ch * s_ch // 2048
    if used < n_rows * qb:
        grads[used:] = jnp.zeros((n_rows * qb - used, 16, 128), BF16)
    others(n_tm, tm, lambda p: tm_copy(
        dp_s.at[p], dp_r.at[p], b_ss.at[2, p], b_rs.at[2, p], p).wait_recv())
    sm_s[0:1] = jnp.sum(jnp.sum(dp_r[...], axis=0), axis=0, keepdims=True) * frame_norm
    sm_r[row] = sm_s[...]

    def rs_row(p, slot):
        return row_copy(
            grads.at[pl.ds(p * qb, qb)], rs_r.at[slot], r_ss.at[0, p], r_rs.at[0, slot], p)

    def small_row(p, slot):
        return row_copy(sm_s, sm_r.at[slot], r_ss.at[1, p], r_rs.at[1, slot], p)

    others(n_rows, row, lambda p: rs_row(p, row).start())
    others(n_rows, row, lambda p: small_row(p, row).start())
    rs_r[row] = grads[pl.ds(row * qb, qb)]

    halo_wait(halo2_s, halo2_r, halo2_ss, halo2_rs)
    put_shifted(cat_s, 0, halo2_r[0, 0], across)
    put_shifted(cat_s, 1, states_own, across)
    put_shifted(cat_s, band + 1, halo2_r[1, 0], across)
    put_shifted(cat_j, 0, halo2_r[0, 1], across)
    put_shifted(cat_j, 1, adj_own, across)
    put_shifted(cat_j, band + 1, halo2_r[1, 1], across)
    acc = gain[...] * frames_own.astype(F32)
    for i in range(3):
        acc = acc + dot_nn(
            cat_s[i : i + band].reshape(cells, 3 * s_ch), out_w[i].reshape(3 * s_ch, ch))
    y_out[0] = acc.astype(BF16).reshape(band, across, ch)
    acc = gain[...] * cot_own.astype(F32)
    for i in range(3):
        for j in range(3):
            window = cat_j[i : i + band, :, j * s_ch : (j + 1) * s_ch].reshape(cells, s_ch)
            acc = acc + dot_nt(window, in_w[2 - i, 2 - j])
    dx_out[0] = acc.astype(BF16).reshape(band, across, ch)

    others(n_rows, row, lambda p: rs_row(p, p).wait_recv())
    others(n_rows, row, lambda p: small_row(p, p).wait_recv())
    quarter[...] = jnp.sum(rs_r[...].astype(F32), axis=0).astype(BF16)
    small = jnp.sum(sm_r[...], axis=0)
    sm2_s[...] = small
    sm2_r[tm] = small
    gdec_out[...] = small[0:1]

    def rs_tm(p, slot):
        return tm_copy(
            quarter.at[pl.ds(p * pp, pp)], rs_t.at[slot], t_ss.at[0, p], t_rs.at[0, slot], p)

    def small_tm(p, slot):
        return tm_copy(sm2_s, sm2_r.at[slot], t_ss.at[1, p], t_rs.at[1, slot], p)

    others(n_tm, tm, lambda p: rs_tm(p, tm).start())
    others(n_tm, tm, lambda p: small_tm(p, tm).start())
    rs_t[tm] = quarter[pl.ds(tm * pp, pp)]
    others(n_tm, tm, lambda p: rs_tm(p, p).wait_recv())
    total = jnp.sum(rs_t[...].astype(F32), axis=0).astype(BF16)
    piece[...] = total
    full[row, tm] = total

    def ag_tm(p, slot):
        return tm_copy(piece, full.at[row, slot], gt_ss.at[p], gt_rs.at[slot], p)

    def ag_row(p, slot):
        return row_copy(full.at[row], full.at[slot], gr_ss.at[p], gr_rs.at[slot], p)

    others(n_tm, tm, lambda p: ag_tm(p, tm).start())
    others(n_tm, tm, lambda p: small_tm(p, p).wait_recv())
    ggain_out[...] = jnp.sum(sm2_r[...], axis=0)[1:2, 0:ch]
    others(n_tm, tm, lambda p: ag_tm(p, p).wait_recv())
    others(n_rows, row, lambda p: ag_row(p, row).start())
    others(n_rows, row, lambda p: ag_row(p, p).wait_recv())

    everything = full[...].reshape(n_rows * qb, 16, 128)
    half = 9 * ch // 16
    for h in range(s_ch // 128):
        gin_out[:, h * 128 : (h + 1) * 128] = (
            everything[h * half : (h + 1) * half].astype(F32).reshape(9 * ch, 128))
    base = 9 * s_ch * ch // 2048
    gout_out[...] = everything[base : 2 * base].astype(F32).reshape(9 * s_ch, ch)

    halo_end(halo_s, halo_r, halo_ss, halo_rs)
    halo_end(halo2_s, halo2_r, halo2_ss, halo2_rs)

    def tm_sends(p):
        tm_copy(dec_s, dec_all.at[tm], dec_ss.at[p], dec_rs.at[tm], p).wait_send()
        tm_copy(st_d.at[p], rc_d.at[tm], a_ss.at[0, p], a_rs.at[0, tm], p).wait_send()
        tm_copy(st_o.at[p], rc_o.at[tm], a_ss.at[1, p], a_rs.at[1, tm], p).wait_send()
        tm_copy(out_s.at[p], got_s.at[tm], b_ss.at[0, p], b_rs.at[0, tm], p).wait_send()
        tm_copy(out_j.at[p], got_j.at[tm], b_ss.at[1, p], b_rs.at[1, tm], p).wait_send()
        tm_copy(dp_s.at[p], dp_r.at[tm], b_ss.at[2, p], b_rs.at[2, tm], p).wait_send()
        rs_tm(p, tm).wait_send()
        small_tm(p, tm).wait_send()
        ag_tm(p, tm).wait_send()

    def row_sends(p):
        rs_row(p, row).wait_send()
        small_row(p, row).wait_send()
        ag_row(p, row).wait_send()

    others(n_tm, tm, tm_sends)
    others(n_rows, row, row_sends)


def on_device(n_tm, n_rows, frames, decays, in_weight, out_weight, skip_gain, cotangent):
    frame_count, band, across, ch = frames.shape
    s_ch = in_weight.shape[3]
    cells = band * across
    assert frame_count == 1 and cells % (8 * n_tm) == 0
    assert ch == 128 and s_ch % 128 == 0 and across % 16 == 0
    cell_norm = 1.0 / math.sqrt(frame_count * n_tm * band * n_rows * across)
    frame_norm = 1.0 / math.sqrt(band * n_rows * across)
    chunk = cells // n_tm
    used = 18 * ch * s_ch // 2048
    pp = -(-used // (n_tm * n_rows))
    vmem = pltpu.VMEM
    parts = lambda kind: vmem((n_tm, chunk, s_ch), kind)
    dma = pltpu.SemaphoreType.DMA
    scratch = [
        vmem((2, 2, across, ch), BF16), vmem((2, 2, across, ch), BF16),
        vmem((8, s_ch), F32), vmem((n_tm, 8, s_ch), F32),
        vmem((band + 2, across, 3 * ch), BF16), vmem((band + 2, across, 3 * ch), BF16),
        parts(BF16), parts(BF16), parts(BF16), parts(BF16),
        vmem((n_tm + 1, chunk, s_ch), F32),
        parts(BF16), parts(BF16),
        vmem((n_tm, 8, s_ch), F32), vmem((n_tm, 8, s_ch), F32),
        parts(BF16), parts(BF16),
        vmem((2, 2, across, s_ch), BF16), vmem((2, 2, across, s_ch), BF16),
        vmem((band + 2, across, 3 * s_ch), BF16), vmem((band + 2, across, 3 * s_ch), BF16),
        vmem((n_rows * n_tm * pp, 16, 128), BF16),
        vmem((n_rows, n_tm * pp, 16, 128), BF16),
        vmem((n_tm * pp, 16, 128), BF16),
        vmem((n_tm, pp, 16, 128), BF16),
        vmem((pp, 16, 128), BF16),
        vmem((n_rows, n_tm, pp, 16, 128), BF16),
        vmem((8, s_ch), F32), vmem((n_rows, 8, s_ch), F32),
        vmem((8, s_ch), F32), vmem((n_tm, 8, s_ch), F32),
        dma((2,)), dma((2,)), dma((2,)), dma((2,)), dma((n_tm,)), dma((n_tm,)),
        dma((2, n_tm)), dma((2, n_tm)), dma((3, n_tm)), dma((3, n_tm)),
        dma((2, n_rows)), dma((2, n_rows)), dma((2, n_tm)), dma((2, n_tm)),
        dma((n_tm,)), dma((n_tm,)), dma((n_rows,)), dma((n_rows,)),
    ]
    y, dx, gin, gout, ggain, gdec = pl.pallas_call(
        functools.partial(kernel, n_tm, n_rows, pp, cell_norm, frame_norm),
        out_shape=(
            jax.ShapeDtypeStruct(frames.shape, BF16),
            jax.ShapeDtypeStruct(frames.shape, BF16),
            jax.ShapeDtypeStruct((9 * ch, s_ch), F32),
            jax.ShapeDtypeStruct((9 * s_ch, ch), F32),
            jax.ShapeDtypeStruct((1, ch), F32),
            jax.ShapeDtypeStruct((1, s_ch), F32),
        ),
        in_specs=[pl.BlockSpec(memory_space=pltpu.VMEM)] * 6,
        out_specs=[pl.BlockSpec(memory_space=pltpu.VMEM)] * 6,
        scratch_shapes=scratch,
        compiler_params=pltpu.CompilerParams(
            collective_id=0, has_side_effects=True, vmem_limit_bytes=48 * 2**20),
    )(frames, decays, in_weight, out_weight, skip_gain.reshape(1, ch), cotangent)
    return (y, dx, gin.reshape(3, 3, ch, s_ch), gout.reshape(3, 3, s_ch, ch),
            ggain.reshape(ch), gdec)


def solution(mesh):
    in_specs = (
        P("tm", "rows", None, None),
        P("tm", None),
        P(),
        P(),
        P(),
        P("tm", "rows", None, None),
    )
    out_specs = (
        P("tm", "rows", None, None),
        P("tm", "rows", None, None),
        P(),
        P(),
        P(),
        P("tm", None),
    )
    body = functools.partial(on_device, mesh.shape["tm"], mesh.shape["rows"])
    return jax.shard_map(
        body, mesh=mesh, in_specs=in_specs, out_specs=out_specs, check_vma=False
    )
```

time: 305 us -> 88.3 us (0.29)
  waiting for transfers between devices: 166 us -> 0 us
  Pallas kernels: 0 us -> 76.9 us
  blocking collectives: 65.8 us -> 0 us
  starting transfers between devices: 20.1 us -> 0 us
  other arithmetic: 15.3 us -> 0 us
  matrix products: 13.9 us -> 0 us
  between operations: 14.4 us -> 0.66 us
    psum x1 -> x0, waiting for transfers between devices: 94 us -> none  [on_device(): lax.psum((in_grad_terms, out_grad_terms, gain_terms), ('tm', 'rows'))]
    pallas_call x0 -> x1, Pallas kernels: none -> 76.9 us  [on_device(): pl.pallas_call(functools.partial(kernel, n_tm, n_rows, pp, cell_norm, fra...]
    all_gather x2 -> x0, waiting for transfers between devices: 71.4 us -> none  [entering(): lax.all_gather(a.astype(kind), axis)]
    psum x2 -> x0, blocking collectives: 45 us -> none  [the longest x1 37.1 us: on_device(): lax.psum((in_grad_terms, out_grad_terms, gain_terms), ('tm', 'rows'))]
    all_gather x1 -> x0, blocking collectives: 20.8 us -> none  [entering(): lax.all_gather(a.astype(kind), axis)]
    ppermute x8 -> x0, starting transfers between devices: 20 us -> none  [the longest x4 14.8 us: padded_2(): lax.ppermute(lax.slice_in_dim(block, block.shape[dim] - width, None, axis...]
    dot_general x54 -> x0, matrix products: 13.9 us -> none  [the longest x36 9.44 us: conv_taps(): jnp.dot(window, weights[row_tap, col_tap], preferred_element_type=jnp.flo...]
    add x7 -> x0, other arithmetic: 8.23 us -> none  [combine(): later[0][None, None, :] * earlier[1] + later[1]]
  transfers between devices with their start and end apart: 11 -> 0, of which waited for: 5 -> 0; matrix products, arithmetic and copies ran while one was open for 3% -> 0% of each run, Pallas kernels for 0% -> 0%
where the time goes in v1:
time: 88.3 us; the launch traced here: 87.2 us
  Pallas kernels  76.9 us (87%)
  local copies, waits for them, and re-layouts  9.67 us (11%)
    pallas_call x1, Pallas kernels, on_device(): pl.pallas_call(functools.partial(kernel, n_tm, n_rows, pp, cell_norm, fra...  76.9 us
    unnamed x18, local copies, waits for them, and re-layouts  9.67 us

profile of v1, /device:TPU:0, one launch (start us, length us, event | category | flops | bytes accessed | tf_op | source)
XLA Modules:
  0.0 87.2 jit_solution(7864232336265281699)
XLA Ops:
  0.6 0.0 copy-start
  0.6 1.1 %copy-done = bf16[3,3,128,256]{3,2,1,0:T(8,128)(2,1)S(1)} copy-done((bf16[3,3,128,256]{3,2,1,0:T(8,128)(2,1)S(1)}, bf16[3,3,128,256]{3,2,1,0:T(8,128)(2,1)}, u32[]{:S(2)}) %copy-start) | copy-done | bytes 589848
  1.7 0.0 copy-start.1
  1.7 1.1 %copy-done.1 = bf16[3,3,256,128]{3,2,1,0:T(8,128)(2,1)S(1)} copy-done((bf16[3,3,256,128]{3,2,1,0:T(8,128)(2,1)S(1)}, bf16[3,3,256,128]{3,2,1,0:T(8,128)(2,1)}, u32[]{:S(2)}) %copy-start.1) | copy-done | bytes 589848
  2.8 0.0 copy-start.2
  2.8 0.9 %copy-done.2 = bf16[1,8,64,128]{3,2,1,0:T(8,128)(2,1)S(1)} copy-done((bf16[1,8,64,128]{3,2,1,0:T(8,128)(2,1)S(1)}, bf16[1,8,64,128]{3,2,1,0:T(8,128)(2,1)}, u32[]{:S(2)}) %copy-start.2) | copy-done | bytes 131096
  3.7 0.0 copy-start.3
  3.7 0.9 %copy-done.3 = bf16[1,8,64,128]{3,2,1,0:T(8,128)(2,1)S(1)} copy-done((bf16[1,8,64,128]{3,2,1,0:T(8,128)(2,1)S(1)}, bf16[1,8,64,128]{3,2,1,0:T(8,128)(2,1)}, u32[]{:S(2)}) %copy-start.3) | copy-done | bytes 131096
  4.6 0.0 copy-start.4
  4.6 0.7 copy-done.4
  5.3 0.0 copy-start.5
  5.3 0.7 copy-done.5
  5.9 76.9 %shard_map.109 = (bf16[1,8,64,128]{3,2,1,0:T(8,128)(2,1)S(1)}, bf16[1,8,64,128]{3,2,1,0:T(8,128)(2,1)S(1)}, f32[1152,256]{1,0:T(8,128)S(1)}, f32[2304,128]{1,0:T...) custom-call(bf16[1,8,64,128]{3,2,1,0:T(8,128)(2,1)S(1)} %copy-done.2, f32[1,256]{1,0:T(1,128)S(1)} %copy-done.4, ...), custom_call_target="tpu_custom_call" | custom-call | tf_op jit(solution)/shard_map/pallas_call | solution.py:386
  82.8 0.7 copy.18
  83.4 0.7 copy.19
  84.1 1.0 %copy.20 = f32[3,3,128,256]{3,2,1,0:T(8,128)} copy(f32[3,3,128,256]{3,2,1,0:T(8,128)S(1)} %bitcast.5) | data formatting | bytes 2359296
  85.1 1.0 %copy.21 = f32[3,3,256,128]{3,2,1,0:T(8,128)} copy(f32[3,3,256,128]{3,2,1,0:T(8,128)S(1)} %bitcast.4) | data formatting | bytes 2359296
  86.1 0.5 copy.22
  86.6 0.6 copy.23
Async XLA Ops:
  0.6 1.1 %copy-start = (bf16[3,3,128,256]{3,2,1,0:T(8,128)(2,1)S(1)}, bf16[3,3,128,256]{3,2,1,0:T(8,128)(2,1)}, u32[]{:S(2)}) copy-start(bf16[3,3,128,256]{3,2,1,0:T(8,128)(2,1)} %in_w.1) | copy-start | bytes 1769476
  1.7 1.1 %copy-start.1 = (bf16[3,3,256,128]{3,2,1,0:T(8,128)(2,1)S(1)}, bf16[3,3,256,128]{3,2,1,0:T(8,128)(2,1)}, u32[]{:S(2)}) copy-start(bf16[3,3,256,128]{3,2,1,0:T(8,128)(2,1)} %out_w.1) | copy-start | bytes 1769476
  2.8 0.9 %copy-start.2 = (bf16[1,8,64,128]{3,2,1,0:T(8,128)(2,1)S(1)}, bf16[1,8,64,128]{3,2,1,0:T(8,128)(2,1)}, u32[]{:S(2)}) copy-start(bf16[1,8,64,128]{3,2,1,0:T(8,128)(2,1)} %frames.1) | copy-start | bytes 393220
  3.7 0.9 %copy-start.3 = (bf16[1,8,64,128]{3,2,1,0:T(8,128)(2,1)S(1)}, bf16[1,8,64,128]{3,2,1,0:T(8,128)(2,1)}, u32[]{:S(2)}) copy-start(bf16[1,8,64,128]{3,2,1,0:T(8,128)(2,1)} %cot.1) | copy-start | bytes 393220
  4.6 0.7 copy-start.4
  5.3 0.7 copy-start.5

commit v2 on v1

--- a/solution.py
+++ b/solution.py
@@ -40,23 +40,32 @@
 
 
 def kernel(
-    n_tm, n_rows, pp, cell_norm, frame_norm,
+    n_tm, n_rows, g, pa, pb, cell_norm, frame_norm,
     frames, decays, in_w, out_w, gain, cot,
     y_out, dx_out, gin_out, gout_out, ggain_out, gdec_out,
     halo_s, halo_r, dec_s, dec_all, cat_f, cat_c,
-    st_d, st_o, rc_d, rc_o, st32, out_s, out_j, dp_s, dp_r, got_s, got_j,
+    st_d, st_o, rc_d, rc_o, st32, ad32, out_s, out_j, dp_s, dp_r, got_s, got_j,
+    cf_s, cf_r, cb_s, cb_r,
     halo2_s, halo2_r, cat_s, cat_j,
-    grads, rs_r, quarter, rs_t, piece, full, sm_s, sm_r, sm2_s, sm2_r,
+    grads, rs_r, quarter, rs_t, piece, full,
+    rb_t, eighth, rb_r, piece_b, full_b, sm_s, sm_r, sm2_s, sm2_r,
     halo_ss, halo_rs, halo2_ss, halo2_rs, dec_ss, dec_rs,
     a_ss, a_rs, b_ss, b_rs, r_ss, r_rs, t_ss, t_rs, gt_ss, gt_rs, gr_ss, gr_rs,
+    bt_ss, bt_rs, br_ss, br_rs, hr_ss, hr_rs, ht_ss, ht_rs, c_ss, c_rs,
 ):
     tm = lax.axis_index("tm")
     row = lax.axis_index("rows")
     _, band, across, ch = frames.shape
     s_ch = in_w.shape[3]
     cells = band * across
-    chunk = cells // n_tm
-    qb = n_tm * pp
+    chunk = cells // g
+    qa = n_tm * pa
+    qb = n_rows * pb
+    na = n_rows * qa
+    groups = n_tm // g
+    group = tm // g
+    me = lax.rem(tm, g)
+    first = group * g
 
     def flat(ref):
         if chunk % 16 == 0:
@@ -75,6 +84,9 @@
             src_ref=src, dst_ref=dst, send_sem=ss, recv_sem=rs,
             device_id={"tm": peer}, device_id_type=MESH,
         )
+
+    def g_copy(src, dst, ss, rs, peer):
+        return tm_copy(src, dst, ss, rs, first + peer)
 
     def row_copy(src, dst, ss, rs, peer):
         return pltpu.make_async_remote_copy(
@@ -137,12 +149,12 @@
     halo_s[1, 1] = cot[0, band - 1]
     own_decay = jnp.broadcast_to(decays[...], (8, s_ch))
     dec_s[...] = own_decay
-    dec_all[tm] = own_decay
+    dec_all[me] = own_decay
     pl.semaphore_wait(barrier, n_tm - 1 + n_rows - 1)
 
     halo_start(halo_s, halo_r, halo_ss, halo_rs)
-    others(n_tm, tm, lambda p: tm_copy(
-        dec_s, dec_all.at[tm], dec_ss.at[p], dec_rs.at[tm], p).start())
+    others(g, me, lambda p: g_copy(
+        dec_s, dec_all.at[me], dec_ss.at[p], dec_rs.at[me], p).start())
 
     frames_own = frames[0].reshape(cells, ch)
     cot_own = cot[0].reshape(cells, ch)
@@ -163,10 +175,10 @@
     for i in range(3):
         term = dot_nn(cat_f[i : i + band].reshape(cells, 3 * ch), in_w[i].reshape(3 * ch, s_ch))
         acc = term if acc is None else acc + term
-    st_d[...] = acc.reshape(n_tm, chunk, s_ch).astype(BF16)
-    others(n_tm, tm, lambda p: tm_copy(
-        st_d.at[p], rc_d.at[tm], a_ss.at[0, p], a_rs.at[0, tm], p).start())
-    rc_d[tm] = st_d[tm]
+    st_d[...] = acc.reshape(g, chunk, s_ch).astype(BF16)
+    others(g, me, lambda p: g_copy(
+        st_d.at[p], rc_d.at[me], a_ss.at[0, p], a_rs.at[0, me], p).start())
+    rc_d[me] = st_d[me]
 
     acc = None
     for i in range(3):
@@ -174,58 +186,157 @@
             window = cat_c[i : i + band, :, j * ch : (j + 1) * ch].reshape(cells, ch)
             term = dot_nt(window, out_w[2 - i, 2 - j])
             acc = term if acc is None else acc + term
-    st_o[...] = acc.reshape(n_tm, chunk, s_ch).astype(BF16)
-    others(n_tm, tm, lambda p: tm_copy(
-        st_o.at[p], rc_o.at[tm], a_ss.at[1, p], a_rs.at[1, tm], p).start())
-    rc_o[tm] = st_o[tm]
-
-    others(n_tm, tm, lambda p: tm_copy(
+    st_o[...] = acc.reshape(g, chunk, s_ch).astype(BF16)
+    others(g, me, lambda p: g_copy(
+        st_o.at[p], rc_o.at[me], a_ss.at[1, p], a_rs.at[1, me], p).start())
+    rc_o[me] = st_o[me]
+
+    others(g, me, lambda p: g_copy(
         dec_s, dec_all.at[p], dec_ss.at[p], dec_rs.at[p], p).wait_recv())
-    others(n_tm, tm, lambda p: tm_copy(
+    others(g, me, lambda p: g_copy(
         st_d.at[p], rc_d.at[p], a_ss.at[0, p], a_rs.at[0, p], p).wait_recv())
+    zero = jnp.zeros((chunk, s_ch), F32)
+
+    def carry_f():
+        return tm_copy(cf_s, cf_r, c_ss.at[0], c_rs.at[0], tm + g)
+
+    def carry_b():
+        return tm_copy(cb_s, cb_r, c_ss.at[1], c_rs.at[1], tm - g)
+
+    has_before = group > 0
+    has_after = group < groups - 1
 
     def forward(t, state):
         state = dec_all[t][0:1] * state + rc_d[t].astype(F32)
         st32[t + 1] = state
+        return state
+
+    state_end = lax.fori_loop(0, g, forward, zero)
+
+    @pl.when(jnp.logical_not(has_before))
+    def _():
+        cf_r[...] = jnp.zeros(cf_r.shape, BF16)
+        if groups > 1:
+            cf_s[...] = state_end.astype(BF16)
+            carry_f().start()
+
+    others(g, me, lambda p: g_copy(
+        st_o.at[p], rc_o.at[p], a_ss.at[1, p], a_rs.at[1, p], p).wait_recv())
+
+    def backward(turn, carried):
+        t = g - 1 - turn
+        adjoint = rc_o[t].astype(F32) + carried
+        ad32[t] = adjoint
+        return dec_all[t][0:1] * adjoint
+
+    adjoint_end = lax.fori_loop(0, g, backward, zero)
+
+    @pl.when(jnp.logical_not(has_after))
+    def _():
+        cb_r[...] = jnp.zeros(cb_r.shape, BF16)
+        if groups > 1:
+            cb_s[...] = adjoint_end.astype(BF16)
+            carry_b().start()
+
+    decay_all = dec_all[0][0:1]
+    for t in range(1, g):
+        decay_all = decay_all * dec_all[t][0:1]
+
+    @pl.when(has_before)
+    def _():
+        tm_copy(cf_s, cf_r, c_ss.at[0], c_rs.at[0], tm - g).wait_recv()
+
+        @pl.when(has_after)
+        def _():
+            cf_s[...] = (st32[g] + decay_all * cf_r[...].astype(F32)).astype(BF16)
+            carry_f().start()
+
+    def forward_fix(t, carried):
+        carried = dec_all[t][0:1] * carried
+        state = st32[t + 1] + carried
+        st32[t + 1] = state
         out_s[t] = state.astype(BF16)
-        return state
-
-    st32[0] = jnp.zeros((chunk, s_ch), F32)
-    lax.fori_loop(0, n_tm, forward, jnp.zeros((chunk, s_ch), F32))
-    others(n_tm, tm, lambda p: tm_copy(
-        out_s.at[p], got_s.at[tm], b_ss.at[0, p], b_rs.at[0, tm], p).start())
-    got_s[tm] = out_s[tm]
-
-    others(n_tm, tm, lambda p: tm_copy(
-        st_o.at[p], rc_o.at[p], a_ss.at[1, p], a_rs.at[1, p], p).wait_recv())
-
-    def backward(turn, carried):
-        t = n_tm - 1 - turn
-        adjoint = rc_o[t].astype(F32) + carried
+        return carried
+
+    state_in = cf_r[...].astype(F32)
+    st32[0] = state_in
+    lax.fori_loop(0, g, forward_fix, state_in)
+    others(g, me, lambda p: g_copy(
+        out_s.at[p], got_s.at[me], b_ss.at[0, p], b_rs.at[0, me], p).start())
+    got_s[me] = out_s[me]
+
+    @pl.when(has_after)
+    def _():
+        tm_copy(cb_s, cb_r, c_ss.at[1], c_rs.at[1], tm + g).wait_recv()
+
+        @pl.when(has_before)
+        def _():
+            cb_s[...] = (
+                dec_all[0][0:1] * ad32[0] + decay_all * cb_r[...].astype(F32)).astype(BF16)
+            carry_b().start()
+
+    def backward_fix(turn, carried):
+        t = g - 1 - turn
+        adjoint = ad32[t] + carried
         out_j[t] = adjoint.astype(BF16)
         dp_s[t] = jnp.sum((adjoint * st32[t]).reshape(chunk // 8, 8, s_ch), axis=0)
-        return dec_all[t][0:1] * adjoint
-
-    lax.fori_loop(0, n_tm, backward, jnp.zeros((chunk, s_ch), F32))
-    others(n_tm, tm, lambda p: tm_copy(
-        out_j.at[p], got_j.at[tm], b_ss.at[1, p], b_rs.at[1, tm], p).start())
-    others(n_tm, tm, lambda p: tm_copy(
-        dp_s.at[p], dp_r.at[tm], b_ss.at[2, p], b_rs.at[2, tm], p).start())
-    got_j[tm] = out_j[tm]
-    dp_r[tm] = dp_s[tm]
-
-    others(n_tm, tm, lambda p: tm_copy(
+        return dec_all[t][0:1] * carried
+
+    lax.fori_loop(0, g, backward_fix, cb_r[...].astype(F32))
+    others(g, me, lambda p: g_copy(
+        out_j.at[p], got_j.at[me], b_ss.at[1, p], b_rs.at[1, me], p).start())
+    others(g, me, lambda p: g_copy(
+        dp_s.at[p], dp_r.at[me], b_ss.at[2, p], b_rs.at[2, me], p).start())
+    got_j[me] = out_j[me]
+    dp_r[me] = dp_s[me]
+
+    def rs_row(p, slot):
+        return row_copy(
+            grads.at[pl.ds(p * qa, qa)], rs_r.at[slot], r_ss.at[0, p], r_rs.at[0, slot], p)
+
+    def small_row(p, slot):
+        return row_copy(sm_s, sm_r.at[slot], r_ss.at[1, p], r_rs.at[1, slot], p)
+
+    def rb_tm(p, slot):
+        return tm_copy(
+            grads.at[pl.ds(na + p * qb, qb)], rb_t.at[slot], bt_ss.at[p], bt_rs.at[slot], p)
+
+    def rb_row(p, slot):
+        return row_copy(
+            eighth.at[pl.ds(p * pb, pb)], rb_r.at[slot], br_ss.at[p], br_rs.at[slot], p)
+
+    def hb_row(p, slot):
+        return row_copy(piece_b, full_b.at[tm, slot], hr_ss.at[p], hr_rs.at[slot], p)
+
+    def hb_tm(p, slot):
+        return tm_copy(full_b.at[tm], full_b.at[slot], ht_ss.at[p], ht_rs.at[slot], p)
+
+    section = 9 * s_ch * ch // 2048
+    early = section // qa
+
+    def rs_early(p):
+        @pl.when(p < early)
+        def _():
+            rs_row(p, row).start()
+
+    def rs_late(p):
+        @pl.when(p >= early)
+        def _():
+            rs_row(p, row).start()
+
+    others(g, me, lambda p: g_copy(
         out_s.at[p], got_s.at[p], b_ss.at[0, p], b_rs.at[0, p], p).wait_recv())
     states_own = flat(got_s)
     for i in range(3):
         value = dot_tn(states_own, cat_c[i : i + band].reshape(cells, 3 * ch)) * cell_norm
         for j in range(3):
             tap = (2 - i) * 3 + 2 - j
-            base = 9 * s_ch * ch // 2048 + tap * (s_ch // 16)
+            base = tap * (s_ch // 16)
             grads[base : base + s_ch // 16] = (
                 value[:, j * ch : (j + 1) * ch].astype(BF16).reshape(s_ch // 16, 16, ch))
-
-    others(n_tm, tm, lambda p: tm_copy(
+    others(n_rows, row, rs_early)
+
+    others(g, me, lambda p: g_copy(
         out_j.at[p], got_j.at[p], b_ss.at[1, p], b_rs.at[1, p], p).wait_recv())
     adj_own = flat(got_j)
     halo2_s[0, 0] = states_own[0:across]
@@ -237,27 +348,20 @@
     for i in range(3):
         value = dot_tn(cat_f[i : i + band].reshape(cells, 3 * ch), adj_own) * cell_norm
         for h in range(s_ch // 128):
-            base = (h * 3 + i) * blocks
+            base = section + (h * 3 + i) * blocks
             grads[base : base + blocks] = (
                 value[:, h * 128 : (h + 1) * 128].astype(BF16).reshape(blocks, 16, 128))
-    used = 18 * ch * s_ch // 2048
-    if used < n_rows * qb:
-        grads[used:] = jnp.zeros((n_rows * qb - used, 16, 128), BF16)
-    others(n_tm, tm, lambda p: tm_copy(
+    if 2 * section < na + n_tm * qb:
+        grads[2 * section :] = jnp.zeros((na + n_tm * qb - 2 * section, 16, 128), BF16)
+    others(n_rows, row, rs_late)
+    others(n_tm, tm, lambda p: rb_tm(p, tm).start())
+    rs_r[row] = grads[pl.ds(row * qa, qa)]
+    rb_t[tm] = grads[pl.ds(na + tm * qb, qb)]
+    others(g, me, lambda p: g_copy(
         dp_s.at[p], dp_r.at[p], b_ss.at[2, p], b_rs.at[2, p], p).wait_recv())
     sm_s[0:1] = jnp.sum(jnp.sum(dp_r[...], axis=0), axis=0, keepdims=True) * frame_norm
     sm_r[row] = sm_s[...]
-
-    def rs_row(p, slot):
-        return row_copy(
-            grads.at[pl.ds(p * qb, qb)], rs_r.at[slot], r_ss.at[0, p], r_rs.at[0, slot], p)
-
-    def small_row(p, slot):
-        return row_copy(sm_s, sm_r.at[slot], r_ss.at[1, p], r_rs.at[1, slot], p)
-
-    others(n_rows, row, lambda p: rs_row(p, row).start())
     others(n_rows, row, lambda p: small_row(p, row).start())
-    rs_r[row] = grads[pl.ds(row * qb, qb)]
 
     halo_wait(halo2_s, halo2_r, halo2_ss, halo2_rs)
     put_shifted(cat_s, 0, halo2_r[0, 0], across)
@@ -288,14 +392,18 @@
 
     def rs_tm(p, slot):
         return tm_copy(
-            quarter.at[pl.ds(p * pp, pp)], rs_t.at[slot], t_ss.at[0, p], t_rs.at[0, slot], p)
+            quarter.at[pl.ds(p * pa, pa)], rs_t.at[slot], t_ss.at[0, p], t_rs.at[0, slot], p)
 
     def small_tm(p, slot):
         return tm_copy(sm2_s, sm2_r.at[slot], t_ss.at[1, p], t_rs.at[1, slot], p)
 
     others(n_tm, tm, lambda p: rs_tm(p, tm).start())
     others(n_tm, tm, lambda p: small_tm(p, tm).start())
-    rs_t[tm] = quarter[pl.ds(tm * pp, pp)]
+    others(n_tm, tm, lambda p: rb_tm(p, p).wait_recv())
+    eighth[...] = jnp.sum(rb_t[...].astype(F32), axis=0).astype(BF16)
+    others(n_rows, row, lambda p: rb_row(p, row).start())
+    rb_r[row] = eighth[pl.ds(row * pb, pb)]
+    rs_t[tm] = quarter[pl.ds(tm * pa, pa)]
     others(n_tm, tm, lambda p: rs_tm(p, p).wait_recv())
     total = jnp.sum(rs_t[...].astype(F32), axis=0).astype(BF16)
     piece[...] = total
@@ -308,39 +416,73 @@
         return row_copy(full.at[row], full.at[slot], gr_ss.at[p], gr_rs.at[slot], p)
 
     others(n_tm, tm, lambda p: ag_tm(p, tm).start())
+    others(n_rows, row, lambda p: rb_row(p, p).wait_recv())
+    total_b = jnp.sum(rb_r[...].astype(F32), axis=0).astype(BF16)
+    piece_b[...] = total_b
+    full_b[tm, row] = total_b
+    others(n_rows, row, lambda p: hb_row(p, row).start())
     others(n_tm, tm, lambda p: small_tm(p, p).wait_recv())
     ggain_out[...] = jnp.sum(sm2_r[...], axis=0)[1:2, 0:ch]
     others(n_tm, tm, lambda p: ag_tm(p, p).wait_recv())
     others(n_rows, row, lambda p: ag_row(p, row).start())
+    others(n_rows, row, lambda p: hb_row(p, p).wait_recv())
+    others(n_tm, tm, lambda p: hb_tm(p, tm).start())
     others(n_rows, row, lambda p: ag_row(p, p).wait_recv())
 
-    everything = full[...].reshape(n_rows * qb, 16, 128)
-    half = 9 * ch // 16
-    for h in range(s_ch // 128):
-        gin_out[:, h * 128 : (h + 1) * 128] = (
-            everything[h * half : (h + 1) * half].astype(F32).reshape(9 * ch, 128))
-    base = 9 * s_ch * ch // 2048
-    gout_out[...] = everything[base : 2 * base].astype(F32).reshape(9 * s_ch, ch)
+    def emit(source, low, high):
+        half = section * 128 // s_ch
+        cuts = [(0, section)] + [
+            (section + h * half, section + (h + 1) * half) for h in range(s_ch // 128)]
+        for which, (begin, end) in enumerate(cuts):
+            a, b = max(begin, low), min(end, high)
+            if a >= b:
+                continue
+            value = source[a - low : b - low].astype(F32).reshape((b - a) * 16, 128)
+            rows = slice((a - begin) * 16, (b - begin) * 16)
+            if which == 0:
+                gout_out[rows, :] = value
+            else:
+                gin_out[rows, (which - 1) * 128 : which * 128] = value
+
+    emit(full[...].reshape(na, 16, 128), 0, na)
+    others(n_tm, tm, lambda p: hb_tm(p, p).wait_recv())
+    emit(full_b[...].reshape(n_tm * qb, 16, 128), na, na + n_tm * qb)
 
     halo_end(halo_s, halo_r, halo_ss, halo_rs)
     halo_end(halo2_s, halo2_r, halo2_ss, halo2_rs)
 
+    if groups > 1:
+        @pl.when(has_after)
+        def _():
+            carry_f().wait_send()
+
+        @pl.when(has_before)
+        def _():
+            carry_b().wait_send()
+
+    def g_sends(p):
+        g_copy(dec_s, dec_all.at[me], dec_ss.at[p], dec_rs.at[me], p).wait_send()
+        g_copy(st_d.at[p], rc_d.at[me], a_ss.at[0, p], a_rs.at[0, me], p).wait_send()
+        g_copy(st_o.at[p], rc_o.at[me], a_ss.at[1, p], a_rs.at[1, me], p).wait_send()
+        g_copy(out_s.at[p], got_s.at[me], b_ss.at[0, p], b_rs.at[0, me], p).wait_send()
+        g_copy(out_j.at[p], got_j.at[me], b_ss.at[1, p], b_rs.at[1, me], p).wait_send()
+        g_copy(dp_s.at[p], dp_r.at[me], b_ss.at[2, p], b_rs.at[2, me], p).wait_send()
+
     def tm_sends(p):
-        tm_copy(dec_s, dec_all.at[tm], dec_ss.at[p], dec_rs.at[tm], p).wait_send()
-        tm_copy(st_d.at[p], rc_d.at[tm], a_ss.at[0, p], a_rs.at[0, tm], p).wait_send()
-        tm_copy(st_o.at[p], rc_o.at[tm], a_ss.at[1, p], a_rs.at[1, tm], p).wait_send()
-        tm_copy(out_s.at[p], got_s.at[tm], b_ss.at[0, p], b_rs.at[0, tm], p).wait_send()
-        tm_copy(out_j.at[p], got_j.at[tm], b_ss.at[1, p], b_rs.at[1, tm], p).wait_send()
-        tm_copy(dp_s.at[p], dp_r.at[tm], b_ss.at[2, p], b_rs.at[2, tm], p).wait_send()
         rs_tm(p, tm).wait_send()
         small_tm(p, tm).wait_send()
         ag_tm(p, tm).wait_send()
+        rb_tm(p, tm).wait_send()
+        hb_tm(p, tm).wait_send()
 
     def row_sends(p):
         rs_row(p, row).wait_send()
         small_row(p, row).wait_send()
         ag_row(p, row).wait_send()
-
+        rb_row(p, row).wait_send()
+        hb_row(p, row).wait_send()
+
+    others(g, me, g_sends)
     others(n_tm, tm, tm_sends)
     others(n_rows, row, row_sends)
 
@@ -349,42 +491,54 @@
     frame_count, band, across, ch = frames.shape
     s_ch = in_weight.shape[3]
     cells = band * across
-    assert frame_count == 1 and cells % (8 * n_tm) == 0
+    assert frame_count == 1 and n_tm % 4 == 0 and cells % 32 == 0
     assert ch == 128 and s_ch % 128 == 0 and across % 16 == 0
     cell_norm = 1.0 / math.sqrt(frame_count * n_tm * band * n_rows * across)
     frame_norm = 1.0 / math.sqrt(band * n_rows * across)
-    chunk = cells // n_tm
+    g = 4
+    chunk = cells // g
+    devices = n_tm * n_rows
     used = 18 * ch * s_ch // 2048
-    pp = -(-used // (n_tm * n_rows))
+    pa = -(-2 * used // (3 * devices))
+    pb = max(1, -(-(used - pa * devices) // devices))
     vmem = pltpu.VMEM
-    parts = lambda kind: vmem((n_tm, chunk, s_ch), kind)
+    parts = lambda kind: vmem((g, chunk, s_ch), kind)
     dma = pltpu.SemaphoreType.DMA
     scratch = [
         vmem((2, 2, across, ch), BF16), vmem((2, 2, across, ch), BF16),
-        vmem((8, s_ch), F32), vmem((n_tm, 8, s_ch), F32),
+        vmem((8, s_ch), F32), vmem((g, 8, s_ch), F32),
         vmem((band + 2, across, 3 * ch), BF16), vmem((band + 2, across, 3 * ch), BF16),
         parts(BF16), parts(BF16), parts(BF16), parts(BF16),
-        vmem((n_tm + 1, chunk, s_ch), F32),
+        vmem((g + 1, chunk, s_ch), F32), parts(F32),
         parts(BF16), parts(BF16),
-        vmem((n_tm, 8, s_ch), F32), vmem((n_tm, 8, s_ch), F32),
+        vmem((g, 8, s_ch), F32), vmem((g, 8, s_ch), F32),
         parts(BF16), parts(BF16),
+        vmem((chunk, s_ch), BF16), vmem((chunk, s_ch), BF16),
+        vmem((chunk, s_ch), BF16), vmem((chunk, s_ch), BF16),
         vmem((2, 2, across, s_ch), BF16), vmem((2, 2, across, s_ch), BF16),
         vmem((band + 2, across, 3 * s_ch), BF16), vmem((band + 2, across, 3 * s_ch), BF16),
-        vmem((n_rows * n_tm * pp, 16, 128), BF16),
-        vmem((n_rows, n_tm * pp, 16, 128), BF16),
-        vmem((n_tm * pp, 16, 128), BF16),
-        vmem((n_tm, pp, 16, 128), BF16),
-        vmem((pp, 16, 128), BF16),
-        vmem((n_rows, n_tm, pp, 16, 128), BF16),
+        vmem((devices * (pa + pb), 16, 128), BF16),
+        vmem((n_rows, n_tm * pa, 16, 128), BF16),
+        vmem((n_tm * pa, 16, 128), BF16),
+        vmem((n_tm, pa, 16, 128), BF16),
+        vmem((pa, 16, 128), BF16),
+        vmem((n_rows, n_tm, pa, 16, 128), BF16),
+        vmem((n_tm, n_rows * pb, 16, 128), BF16),
+        vmem((n_rows * pb, 16, 128), BF16),
+        vmem((n_rows, pb, 16, 128), BF16),
+        vmem((pb, 16, 128), BF16),
+        vmem((n_tm, n_rows, pb, 16, 128), BF16),
         vmem((8, s_ch), F32), vmem((n_rows, 8, s_ch), F32),
         vmem((8, s_ch), F32), vmem((n_tm, 8, s_ch), F32),
-        dma((2,)), dma((2,)), dma((2,)), dma((2,)), dma((n_tm,)), dma((n_tm,)),
-        dma((2, n_tm)), dma((2, n_tm)), dma((3, n_tm)), dma((3, n_tm)),
+        dma((2,)), dma((2,)), dma((2,)), dma((2,)), dma((g,)), dma((g,)),
+        dma((2, g)), dma((2, g)), dma((3, g)), dma((3, g)),
         dma((2, n_rows)), dma((2, n_rows)), dma((2, n_tm)), dma((2, n_tm)),
         dma((n_tm,)), dma((n_tm,)), dma((n_rows,)), dma((n_rows,)),
+        dma((n_tm,)), dma((n_tm,)), dma((n_rows,)), dma((n_rows,)),
+        dma((n_rows,)), dma((n_rows,)), dma((n_tm,)), dma((n_tm,)), dma((2,)), dma((2,)),
     ]
     y, dx, gin, gout, ggain, gdec = pl.pallas_call(
-        functools.partial(kernel, n_tm, n_rows, pp, cell_norm, frame_norm),
+        functools.partial(kernel, n_tm, n_rows, g, pa, pb, cell_norm, frame_norm),
         out_shape=(
             jax.ShapeDtypeStruct(frames.shape, BF16),
             jax.ShapeDtypeStruct(frames.shape, BF16),

time: 88.3 us -> 67.5 us (0.76)
  Pallas kernels: 76.9 us -> 56.9 us
    pallas_call x1, Pallas kernels: 76.9 us -> 56.9 us  [on_device(): pl.pallas_call(functools.partial(kernel, n_tm, n_rows, g, pa, pb, cell_no...]
where the time goes in v2:
time: 67.5 us; the launch traced here: 67.2 us
  Pallas kernels  56.9 us (84%)
  local copies, waits for them, and re-layouts  9.67 us (14%)
    pallas_call x1, Pallas kernels, on_device(): pl.pallas_call(functools.partial(kernel, n_tm, n_rows, g, pa, pb, cell_no...  56.9 us
    unnamed x18, local copies, waits for them, and re-layouts  9.67 us

profile of v2, /device:TPU:0, one launch (start us, length us, event | category | flops | bytes accessed | tf_op | source)
XLA Modules:
  0.0 67.2 jit_solution(5597702936487398029)
XLA Ops:
  0.6 0.0 copy-start
  0.6 1.1 %copy-done = bf16[3,3,128,256]{3,2,1,0:T(8,128)(2,1)S(1)} copy-done((bf16[3,3,128,256]{3,2,1,0:T(8,128)(2,1)S(1)}, bf16[3,3,128,256]{3,2,1,0:T(8,128)(2,1)}, u32[]{:S(2)}) %copy-start) | copy-done | bytes 589848
  1.7 0.0 copy-start.1
  1.7 1.1 %copy-done.1 = bf16[3,3,256,128]{3,2,1,0:T(8,128)(2,1)S(1)} copy-done((bf16[3,3,256,128]{3,2,1,0:T(8,128)(2,1)S(1)}, bf16[3,3,256,128]{3,2,1,0:T(8,128)(2,1)}, u32[]{:S(2)}) %copy-start.1) | copy-done | bytes 589848
  2.8 0.0 copy-start.2
  2.8 0.9 %copy-done.2 = bf16[1,8,64,128]{3,2,1,0:T(8,128)(2,1)S(1)} copy-done((bf16[1,8,64,128]{3,2,1,0:T(8,128)(2,1)S(1)}, bf16[1,8,64,128]{3,2,1,0:T(8,128)(2,1)}, u32[]{:S(2)}) %copy-start.2) | copy-done | bytes 131096
  3.7 0.0 copy-start.3
  3.7 0.9 %copy-done.3 = bf16[1,8,64,128]{3,2,1,0:T(8,128)(2,1)S(1)} copy-done((bf16[1,8,64,128]{3,2,1,0:T(8,128)(2,1)S(1)}, bf16[1,8,64,128]{3,2,1,0:T(8,128)(2,1)}, u32[]{:S(2)}) %copy-start.3) | copy-done | bytes 131096
  4.6 0.0 copy-start.4
  4.6 0.7 %copy-done.4 = f32[1,256]{1,0:T(1,128)S(1)} copy-done((f32[1,256]{1,0:T(1,128)S(1)}, f32[1,256]{1,0:T(1,128)}, u32[]{:S(2)}) %copy-start.4) | copy-done | bytes 1048
  5.3 0.0 copy-start.5
  5.3 0.7 copy-done.5
  5.9 56.9 %shard_map.109 = (bf16[1,8,64,128]{3,2,1,0:T(8,128)(2,1)S(1)}, bf16[1,8,64,128]{3,2,1,0:T(8,128)(2,1)S(1)}, f32[1152,256]{1,0:T(8,128)S(1)}, f32[2304,128]{1,0:T...) custom-call(bf16[1,8,64,128]{3,2,1,0:T(8,128)(2,1)S(1)} %copy-done.2, f32[1,256]{1,0:T(1,128)S(1)} %copy-done.4, ...), custom_call_target="tpu_custom_call" | custom-call | tf_op jit(solution)/shard_map/pallas_call | solution.py:540
  62.8 0.7 copy.18
  63.4 0.7 copy.19
  64.1 1.0 %copy.20 = f32[3,3,128,256]{3,2,1,0:T(8,128)} copy(f32[3,3,128,256]{3,2,1,0:T(8,128)S(1)} %bitcast.5) | data formatting | bytes 2359296
  65.1 1.0 %copy.21 = f32[3,3,256,128]{3,2,1,0:T(8,128)} copy(f32[3,3,256,128]{3,2,1,0:T(8,128)S(1)} %bitcast.4) | data formatting | bytes 2359296
  66.1 0.5 copy.22
  66.6 0.6 copy.23
Async XLA Ops:
  0.6 1.1 %copy-start = (bf16[3,3,128,256]{3,2,1,0:T(8,128)(2,1)S(1)}, bf16[3,3,128,256]{3,2,1,0:T(8,128)(2,1)}, u32[]{:S(2)}) copy-start(bf16[3,3,128,256]{3,2,1,0:T(8,128)(2,1)} %in_w.1) | copy-start | bytes 1769476
  1.7 1.1 %copy-start.1 = (bf16[3,3,256,128]{3,2,1,0:T(8,128)(2,1)S(1)}, bf16[3,3,256,128]{3,2,1,0:T(8,128)(2,1)}, u32[]{:S(2)}) copy-start(bf16[3,3,256,128]{3,2,1,0:T(8,128)(2,1)} %out_w.1) | copy-start | bytes 1769476
  2.8 0.9 %copy-start.2 = (bf16[1,8,64,128]{3,2,1,0:T(8,128)(2,1)S(1)}, bf16[1,8,64,128]{3,2,1,0:T(8,128)(2,1)}, u32[]{:S(2)}) copy-start(bf16[1,8,64,128]{3,2,1,0:T(8,128)(2,1)} %frames.1) | copy-start | bytes 393220
  3.7 0.9 %copy-start.3 = (bf16[1,8,64,128]{3,2,1,0:T(8,128)(2,1)S(1)}, bf16[1,8,64,128]{3,2,1,0:T(8,128)(2,1)}, u32[]{:S(2)}) copy-start(bf16[1,8,64,128]{3,2,1,0:T(8,128)(2,1)} %cot.1) | copy-start | bytes 393220
  4.6 0.7 %copy-start.4 = (f32[1,256]{1,0:T(1,128)S(1)}, f32[1,256]{1,0:T(1,128)}, u32[]{:S(2)}) copy-start(f32[1,256]{1,0:T(1,128)} %decays.1) | copy-start | bytes 3076
  5.3 0.7 copy-start.5

commit v3 on v2

--- a/solution.py
+++ b/solution.py
@@ -485,6 +485,15 @@
     others(g, me, g_sends)
     others(n_tm, tm, tm_sends)
     others(n_rows, row, row_sends)
+
+
+def write_out(*refs):
+    sem = refs[12]
+    copies = [pltpu.make_async_copy(refs[i], refs[6 + i], sem.at[i]) for i in range(6)]
+    for copy in copies:
+        copy.start()
+    for copy in copies:
+        copy.wait()
 
 
 def on_device(n_tm, n_rows, frames, decays, in_weight, out_weight, skip_gain, cotangent):
@@ -537,7 +546,7 @@
         dma((n_tm,)), dma((n_tm,)), dma((n_rows,)), dma((n_rows,)),
         dma((n_rows,)), dma((n_rows,)), dma((n_tm,)), dma((n_tm,)), dma((2,)), dma((2,)),
     ]
-    y, dx, gin, gout, ggain, gdec = pl.pallas_call(
+    results = pl.pallas_call(
         functools.partial(kernel, n_tm, n_rows, g, pa, pb, cell_norm, frame_norm),
         out_shape=(
             jax.ShapeDtypeStruct(frames.shape, BF16),
@@ -553,6 +562,14 @@
         compiler_params=pltpu.CompilerParams(
             collective_id=0, has_side_effects=True, vmem_limit_bytes=48 * 2**20),
     )(frames, decays, in_weight, out_weight, skip_gain.reshape(1, ch), cotangent)
+    y, dx, gin, gout, ggain, gdec = pl.pallas_call(
+        write_out,
+        out_shape=tuple(jax.ShapeDtypeStruct(a.shape, a.dtype) for a in results),
+        in_specs=[pl.BlockSpec(memory_space=pltpu.VMEM)] * 6,
+        out_specs=[pl.BlockSpec(memory_space=pl.ANY)] * 6,
+        scratch_shapes=[dma((6,))],
+        compiler_params=pltpu.CompilerParams(vmem_limit_bytes=2**20),
+    )(*results)
     return (y, dx, gin.reshape(3, 3, ch, s_ch), gout.reshape(3, 3, s_ch, ch),
             ggain.reshape(ch), gdec)
 

time: 67.5 us -> 64.6 us (0.957)
  local copies, waits for them, and re-layouts: 9.67 us -> 5.26 us
  Pallas kernels: 56.9 us -> 58.4 us
    unnamed x18 -> x12, local copies, waits for them, and re-layouts: 9.67 us -> 5.26 us
    pallas_call x0 -> x1, Pallas kernels: none -> 1.55 us  [on_device(): pl.pallas_call(write_out, out_shape=tuple((jax.ShapeDtypeStruct(a.shape,...]
where the time goes in v3:
time: 64.6 us; the launch traced here: 64.3 us
  Pallas kernels  58.4 us (90%)
  local copies, waits for them, and re-layouts  5.26 us (8%)
  between operations  0.66 us (1%)
    pallas_call x1, Pallas kernels, on_device(): pl.pallas_call(functools.partial(kernel, n_tm, n_rows, g, pa, pb, cell_no...  56.9 us
    unnamed x12, local copies, waits for them, and re-layouts  5.26 us
    pallas_call x1, Pallas kernels, on_device(): pl.pallas_call(write_out, out_shape=tuple((jax.ShapeDtypeStruct(a.shape,...  1.55 us

profile of v3, /device:TPU:0, one launch (start us, length us, event | category | flops | bytes accessed | tf_op | source)
XLA Modules:
  0.0 64.3 jit_solution(9826308097033384281)
XLA Ops:
  0.6 0.0 copy-start
  0.6 1.1 %copy-done = bf16[3,3,128,256]{3,2,1,0:T(8,128)(2,1)S(1)} copy-done((bf16[3,3,128,256]{3,2,1,0:T(8,128)(2,1)S(1)}, bf16[3,3,128,256]{3,2,1,0:T(8,128)(2,1)}, u32[]{:S(2)}) %copy-start) | copy-done | bytes 589848
  1.7 0.0 copy-start.1
  1.7 1.1 %copy-done.1 = bf16[3,3,256,128]{3,2,1,0:T(8,128)(2,1)S(1)} copy-done((bf16[3,3,256,128]{3,2,1,0:T(8,128)(2,1)S(1)}, bf16[3,3,256,128]{3,2,1,0:T(8,128)(2,1)}, u32[]{:S(2)}) %copy-start.1) | copy-done | bytes 589848
  2.8 0.0 copy-start.2
  2.8 0.9 %copy-done.2 = bf16[1,8,64,128]{3,2,1,0:T(8,128)(2,1)S(1)} copy-done((bf16[1,8,64,128]{3,2,1,0:T(8,128)(2,1)S(1)}, bf16[1,8,64,128]{3,2,1,0:T(8,128)(2,1)}, u32[]{:S(2)}) %copy-start.2) | copy-done | bytes 131096
  3.7 0.0 copy-start.3
  3.7 0.9 %copy-done.3 = bf16[1,8,64,128]{3,2,1,0:T(8,128)(2,1)S(1)} copy-done((bf16[1,8,64,128]{3,2,1,0:T(8,128)(2,1)S(1)}, bf16[1,8,64,128]{3,2,1,0:T(8,128)(2,1)}, u32[]{:S(2)}) %copy-start.3) | copy-done | bytes 131096
  4.6 0.0 copy-start.4
  4.6 0.7 %copy-done.4 = f32[1,256]{1,0:T(1,128)S(1)} copy-done((f32[1,256]{1,0:T(1,128)S(1)}, f32[1,256]{1,0:T(1,128)}, u32[]{:S(2)}) %copy-start.4) | copy-done | bytes 1048
  5.3 0.0 copy-start.5
  5.3 0.7 %copy-done.5 = f32[128]{0:T(128)S(1)} copy-done((f32[128]{0:T(128)S(1)}, f32[128]{0:T(128)}, u32[]{:S(2)}) %copy-start.5) | copy-done | bytes 536
  5.9 56.9 %shard_map.109 = (bf16[1,8,64,128]{3,2,1,0:T(8,128)(2,1)S(1)}, bf16[1,8,64,128]{3,2,1,0:T(8,128)(2,1)S(1)}, f32[1152,256]{1,0:T(8,128)S(1)}, f32[2304,128]{1,0:T...) custom-call(bf16[1,8,64,128]{3,2,1,0:T(8,128)(2,1)S(1)} %copy-done.2, f32[1,256]{1,0:T(1,128)S(1)} %copy-done.4, ...), custom_call_target="tpu_custom_call" | custom-call | tf_op jit(solution)/shard_map/pallas_call | solution.py:549
  62.8 1.5 %shard_map.110 = (bf16[1,8,64,128]{3,2,1,0:T(8,128)(2,1)}, bf16[1,8,64,128]{3,2,1,0:T(8,128)(2,1)}, f32[1152,256]{1,0:T(8,128)}, f32[2304,128]{1,0:T(8,128)}, f32[1,128]{1,0:T(1,128)}, /*index=5*/f32[1,256]{1,0:T(1,128)}) custom-call(bf16[1,8,64,128]{3,2,1,0:T(8,128)(2,1)S(1)} %get-tuple-element.18.refs_0_, ...), custom_call_target="tpu_custom_call" | custom-call | tf_op jit(solution)/shard_map/pallas_call | solution.py:565
Async XLA Ops:
  0.6 1.1 %copy-start = (bf16[3,3,128,256]{3,2,1,0:T(8,128)(2,1)S(1)}, bf16[3,3,128,256]{3,2,1,0:T(8,128)(2,1)}, u32[]{:S(2)}) copy-start(bf16[3,3,128,256]{3,2,1,0:T(8,128)(2,1)} %in_w.1) | copy-start | bytes 1769476
  1.7 1.1 %copy-start.1 = (bf16[3,3,256,128]{3,2,1,0:T(8,128)(2,1)S(1)}, bf16[3,3,256,128]{3,2,1,0:T(8,128)(2,1)}, u32[]{:S(2)}) copy-start(bf16[3,3,256,128]{3,2,1,0:T(8,128)(2,1)} %out_w.1) | copy-start | bytes 1769476
  2.8 0.9 %copy-start.2 = (bf16[1,8,64,128]{3,2,1,0:T(8,128)(2,1)S(1)}, bf16[1,8,64,128]{3,2,1,0:T(8,128)(2,1)}, u32[]{:S(2)}) copy-start(bf16[1,8,64,128]{3,2,1,0:T(8,128)(2,1)} %frames.1) | copy-start | bytes 393220
  3.7 0.9 %copy-start.3 = (bf16[1,8,64,128]{3,2,1,0:T(8,128)(2,1)S(1)}, bf16[1,8,64,128]{3,2,1,0:T(8,128)(2,1)}, u32[]{:S(2)}) copy-start(bf16[1,8,64,128]{3,2,1,0:T(8,128)(2,1)} %cot.1) | copy-start | bytes 393220
  4.6 0.7 %copy-start.4 = (f32[1,256]{1,0:T(1,128)S(1)}, f32[1,256]{1,0:T(1,128)}, u32[]{:S(2)}) copy-start(f32[1,256]{1,0:T(1,128)} %decays.1) | copy-start | bytes 3076
  5.3 0.7 %copy-start.5 = (f32[128]{0:T(128)S(1)}, f32[128]{0:T(128)}, u32[]{:S(2)}) copy-start(f32[128]{0:T(128)} %param.10) | copy-start | bytes 1540

commit v4 on v3

--- a/solution.py
+++ b/solution.py
@@ -412,10 +412,15 @@
     def ag_tm(p, slot):
         return tm_copy(piece, full.at[row, slot], gt_ss.at[p], gt_rs.at[slot], p)
 
-    def ag_row(p, slot):
-        return row_copy(full.at[row], full.at[slot], gr_ss.at[p], gr_rs.at[slot], p)
+    def ag_row(q, p, slot):
+        return row_copy(
+            full.at[row, q], full.at[slot, q], gr_ss.at[q, p], gr_rs.at[q, slot], p)
+
+    def forward_piece(q):
+        others(n_rows, row, lambda p: ag_row(q, p, row).start())
 
     others(n_tm, tm, lambda p: ag_tm(p, tm).start())
+    forward_piece(tm)
     others(n_rows, row, lambda p: rb_row(p, p).wait_recv())
     total_b = jnp.sum(rb_r[...].astype(F32), axis=0).astype(BF16)
     piece_b[...] = total_b
@@ -423,11 +428,20 @@
     others(n_rows, row, lambda p: hb_row(p, row).start())
     others(n_tm, tm, lambda p: small_tm(p, p).wait_recv())
     ggain_out[...] = jnp.sum(sm2_r[...], axis=0)[1:2, 0:ch]
-    others(n_tm, tm, lambda p: ag_tm(p, p).wait_recv())
-    others(n_rows, row, lambda p: ag_row(p, row).start())
     others(n_rows, row, lambda p: hb_row(p, p).wait_recv())
     others(n_tm, tm, lambda p: hb_tm(p, tm).start())
-    others(n_rows, row, lambda p: ag_row(p, p).wait_recv())
+
+    def pass_on(q):
+        ag_tm(q, q).wait_recv()
+        forward_piece(q)
+
+    others(n_tm, tm, pass_on)
+
+    def piece_wait(q, carry):
+        others(n_rows, row, lambda p: ag_row(q, p, p).wait_recv())
+        return carry
+
+    lax.fori_loop(0, n_tm, piece_wait, 0)
 
     def emit(source, low, high):
         half = section * 128 // s_ch
@@ -478,13 +492,18 @@
     def row_sends(p):
         rs_row(p, row).wait_send()
         small_row(p, row).wait_send()
-        ag_row(p, row).wait_send()
         rb_row(p, row).wait_send()
         hb_row(p, row).wait_send()
 
     others(g, me, g_sends)
     others(n_tm, tm, tm_sends)
     others(n_rows, row, row_sends)
+
+    def piece_sends(q, carry):
+        others(n_rows, row, lambda p: ag_row(q, p, row).wait_send())
+        return carry
+
+    lax.fori_loop(0, n_tm, piece_sends, 0)
 
 
 def write_out(*refs):
@@ -542,7 +561,7 @@
         dma((2,)), dma((2,)), dma((2,)), dma((2,)), dma((g,)), dma((g,)),
         dma((2, g)), dma((2, g)), dma((3, g)), dma((3, g)),
         dma((2, n_rows)), dma((2, n_rows)), dma((2, n_tm)), dma((2, n_tm)),
-        dma((n_tm,)), dma((n_tm,)), dma((n_rows,)), dma((n_rows,)),
+        dma((n_tm,)), dma((n_tm,)), dma((n_tm, n_rows)), dma((n_tm, n_rows)),
         dma((n_tm,)), dma((n_tm,)), dma((n_rows,)), dma((n_rows,)),
         dma((n_rows,)), dma((n_rows,)), dma((n_tm,)), dma((n_tm,)), dma((2,)), dma((2,)),
     ]

time: 64.6 us -> 63 us (0.975)
  Pallas kernels: 58.4 us -> 56.8 us
    pallas_call x1, Pallas kernels: 56.9 us -> 55.3 us  [on_device(): pl.pallas_call(functools.partial(kernel, n_tm, n_rows, g, pa, pb, cell_no...]
where the time goes in v4:
time: 63 us; the launch traced here: 62.7 us
  Pallas kernels  56.8 us (90%)
  local copies, waits for them, and re-layouts  5.26 us (8%)
  between operations  0.66 us (1%)
    pallas_call x1, Pallas kernels, on_device(): pl.pallas_call(functools.partial(kernel, n_tm, n_rows, g, pa, pb, cell_no...  55.3 us
    unnamed x12, local copies, waits for them, and re-layouts  5.26 us
    pallas_call x1, Pallas kernels, on_device(): pl.pallas_call(write_out, out_shape=tuple((jax.ShapeDtypeStruct(a.shape,...  1.55 us

profile of v4, /device:TPU:0, one launch (start us, length us, event | category | flops | bytes accessed | tf_op | source)
XLA Modules:
  0.0 62.7 jit_solution(10512522523066702431)
XLA Ops:
  0.6 0.0 copy-start
  0.6 1.1 %copy-done = bf16[3,3,128,256]{3,2,1,0:T(8,128)(2,1)S(1)} copy-done((bf16[3,3,128,256]{3,2,1,0:T(8,128)(2,1)S(1)}, bf16[3,3,128,256]{3,2,1,0:T(8,128)(2,1)}, u32[]{:S(2)}) %copy-start) | copy-done | bytes 589848
  1.7 0.0 copy-start.1
  1.7 1.1 %copy-done.1 = bf16[3,3,256,128]{3,2,1,0:T(8,128)(2,1)S(1)} copy-done((bf16[3,3,256,128]{3,2,1,0:T(8,128)(2,1)S(1)}, bf16[3,3,256,128]{3,2,1,0:T(8,128)(2,1)}, u32[]{:S(2)}) %copy-start.1) | copy-done | bytes 589848
  2.8 0.0 copy-start.2
  2.8 0.9 %copy-done.2 = bf16[1,8,64,128]{3,2,1,0:T(8,128)(2,1)S(1)} copy-done((bf16[1,8,64,128]{3,2,1,0:T(8,128)(2,1)S(1)}, bf16[1,8,64,128]{3,2,1,0:T(8,128)(2,1)}, u32[]{:S(2)}) %copy-start.2) | copy-done | bytes 131096
  3.7 0.0 copy-start.3
  3.7 0.9 %copy-done.3 = bf16[1,8,64,128]{3,2,1,0:T(8,128)(2,1)S(1)} copy-done((bf16[1,8,64,128]{3,2,1,0:T(8,128)(2,1)S(1)}, bf16[1,8,64,128]{3,2,1,0:T(8,128)(2,1)}, u32[]{:S(2)}) %copy-start.3) | copy-done | bytes 131096
  4.6 0.0 copy-start.4
  4.6 0.7 %copy-done.4 = f32[1,256]{1,0:T(1,128)S(1)} copy-done((f32[1,256]{1,0:T(1,128)S(1)}, f32[1,256]{1,0:T(1,128)}, u32[]{:S(2)}) %copy-start.4) | copy-done | bytes 1048
  5.3 0.0 copy-start.5
  5.3 0.7 %copy-done.5 = f32[128]{0:T(128)S(1)} copy-done((f32[128]{0:T(128)S(1)}, f32[128]{0:T(128)}, u32[]{:S(2)}) %copy-start.5) | copy-done | bytes 536
  5.9 55.3 %shard_map.109 = (bf16[1,8,64,128]{3,2,1,0:T(8,128)(2,1)S(1)}, bf16[1,8,64,128]{3,2,1,0:T(8,128)(2,1)S(1)}, f32[1152,256]{1,0:T(8,128)S(1)}, f32[2304,128]{1,0:T...) custom-call(bf16[1,8,64,128]{3,2,1,0:T(8,128)(2,1)S(1)} %copy-done.2, f32[1,256]{1,0:T(1,128)S(1)} %copy-done.4, ...), custom_call_target="tpu_custom_call" | custom-call | tf_op jit(solution)/shard_map/pallas_call | solution.py:568
  61.2 1.5 %shard_map.110 = (bf16[1,8,64,128]{3,2,1,0:T(8,128)(2,1)}, bf16[1,8,64,128]{3,2,1,0:T(8,128)(2,1)}, f32[1152,256]{1,0:T(8,128)}, f32[2304,128]{1,0:T(8,128)}, f32[1,128]{1,0:T(1,128)}, /*index=5*/f32[1,256]{1,0:T(1,128)}) custom-call(bf16[1,8,64,128]{3,2,1,0:T(8,128)(2,1)S(1)} %get-tuple-element.18.refs_0_, ...), custom_call_target="tpu_custom_call" | custom-call | tf_op jit(solution)/shard_map/pallas_call | solution.py:584
Async XLA Ops:
  0.6 1.1 %copy-start = (bf16[3,3,128,256]{3,2,1,0:T(8,128)(2,1)S(1)}, bf16[3,3,128,256]{3,2,1,0:T(8,128)(2,1)}, u32[]{:S(2)}) copy-start(bf16[3,3,128,256]{3,2,1,0:T(8,128)(2,1)} %in_w.1) | copy-start | bytes 1769476
  1.7 1.1 %copy-start.1 = (bf16[3,3,256,128]{3,2,1,0:T(8,128)(2,1)S(1)}, bf16[3,3,256,128]{3,2,1,0:T(8,128)(2,1)}, u32[]{:S(2)}) copy-start(bf16[3,3,256,128]{3,2,1,0:T(8,128)(2,1)} %out_w.1) | copy-start | bytes 1769476
  2.8 0.9 %copy-start.2 = (bf16[1,8,64,128]{3,2,1,0:T(8,128)(2,1)S(1)}, bf16[1,8,64,128]{3,2,1,0:T(8,128)(2,1)}, u32[]{:S(2)}) copy-start(bf16[1,8,64,128]{3,2,1,0:T(8,128)(2,1)} %frames.1) | copy-start | bytes 393220
  3.7 0.9 %copy-start.3 = (bf16[1,8,64,128]{3,2,1,0:T(8,128)(2,1)S(1)}, bf16[1,8,64,128]{3,2,1,0:T(8,128)(2,1)}, u32[]{:S(2)}) copy-start(bf16[1,8,64,128]{3,2,1,0:T(8,128)(2,1)} %cot.1) | copy-start | bytes 393220
  4.6 0.7 %copy-start.4 = (f32[1,256]{1,0:T(1,128)S(1)}, f32[1,256]{1,0:T(1,128)}, u32[]{:S(2)}) copy-start(f32[1,256]{1,0:T(1,128)} %decays.1) | copy-start | bytes 3076
  5.3 0.7 %copy-start.5 = (f32[128]{0:T(128)S(1)}, f32[128]{0:T(128)}, u32[]{:S(2)}) copy-start(f32[128]{0:T(128)} %param.10) | copy-start | bytes 1540

commit v5 on v4

--- a/solution.py
+++ b/solution.py
@@ -527,7 +527,7 @@
     chunk = cells // g
     devices = n_tm * n_rows
     used = 18 * ch * s_ch // 2048
-    pa = -(-2 * used // (3 * devices))
+    pa = -(-7 * used // (9 * devices))
     pb = max(1, -(-(used - pa * devices) // devices))
     vmem = pltpu.VMEM
     parts = lambda kind: vmem((g, chunk, s_ch), kind)

time: 63 us -> 69.7 us (1.11)
  the two profiles are of different devices: /device:TPU:0 before, /device:TPU:27 now
where the time goes in v5:
time: 69.7 us; the launch traced here: 69.5 us
  Pallas kernels  63.5 us (91%)
  local copies, waits for them, and re-layouts  5.26 us (8%)
    pallas_call x1, Pallas kernels, on_device(): pl.pallas_call(functools.partial(kernel, n_tm, n_rows, g, pa, pb, cell_no...  62 us
    unnamed x12, local copies, waits for them, and re-layouts  5.26 us
    pallas_call x1, Pallas kernels, on_device(): pl.pallas_call(write_out, out_shape=tuple((jax.ShapeDtypeStruct(a.shape,...  1.55 us

profile of v5, /device:TPU:27, one launch (start us, length us, event | category | flops | bytes accessed | tf_op | source)
XLA Modules:
  0.0 69.5 jit_solution(4519249312754217993)
XLA Ops:
  0.6 0.0 copy-start
  0.6 1.1 %copy-done = bf16[3,3,128,256]{3,2,1,0:T(8,128)(2,1)S(1)} copy-done((bf16[3,3,128,256]{3,2,1,0:T(8,128)(2,1)S(1)}, bf16[3,3,128,256]{3,2,1,0:T(8,128)(2,1)}, u32[]{:S(2)}) %copy-start) | copy-done | bytes 589848
  1.7 0.0 copy-start.1
  1.7 1.1 %copy-done.1 = bf16[3,3,256,128]{3,2,1,0:T(8,128)(2,1)S(1)} copy-done((bf16[3,3,256,128]{3,2,1,0:T(8,128)(2,1)S(1)}, bf16[3,3,256,128]{3,2,1,0:T(8,128)(2,1)}, u32[]{:S(2)}) %copy-start.1) | copy-done | bytes 589848
  2.8 0.0 copy-start.2
  2.8 0.9 %copy-done.2 = bf16[1,8,64,128]{3,2,1,0:T(8,128)(2,1)S(1)} copy-done((bf16[1,8,64,128]{3,2,1,0:T(8,128)(2,1)S(1)}, bf16[1,8,64,128]{3,2,1,0:T(8,128)(2,1)}, u32[]{:S(2)}) %copy-start.2) | copy-done | bytes 131096
  3.7 0.0 copy-start.3
  3.7 0.9 %copy-done.3 = bf16[1,8,64,128]{3,2,1,0:T(8,128)(2,1)S(1)} copy-done((bf16[1,8,64,128]{3,2,1,0:T(8,128)(2,1)S(1)}, bf16[1,8,64,128]{3,2,1,0:T(8,128)(2,1)}, u32[]{:S(2)}) %copy-start.3) | copy-done | bytes 131096
  4.6 0.0 copy-start.4
  4.6 0.7 copy-done.4
  5.3 0.0 copy-start.5
  5.3 0.7 copy-done.5
  5.9 62.0 %shard_map.109 = (bf16[1,8,64,128]{3,2,1,0:T(8,128)(2,1)S(1)}, bf16[1,8,64,128]{3,2,1,0:T(8,128)(2,1)S(1)}, f32[1152,256]{1,0:T(8,128)S(1)}, f32[2304,128]{1,0:T...) custom-call(bf16[1,8,64,128]{3,2,1,0:T(8,128)(2,1)S(1)} %copy-done.2, f32[1,256]{1,0:T(1,128)S(1)} %copy-done.4, ...), custom_call_target="tpu_custom_call" | custom-call | tf_op jit(solution)/shard_map/pallas_call | solution.py:568
  67.9 1.5 %shard_map.110 = (bf16[1,8,64,128]{3,2,1,0:T(8,128)(2,1)}, bf16[1,8,64,128]{3,2,1,0:T(8,128)(2,1)}, f32[1152,256]{1,0:T(8,128)}, f32[2304,128]{1,0:T(8,128)}, f32[1,128]{1,0:T(1,128)}, /*index=5*/f32[1,256]{1,0:T(1,128)}) custom-call(bf16[1,8,64,128]{3,2,1,0:T(8,128)(2,1)S(1)} %get-tuple-element.18.refs_0_, ...), custom_call_target="tpu_custom_call" | custom-call | tf_op jit(solution)/shard_map/pallas_call | solution.py:584
Async XLA Ops:
  0.6 1.1 %copy-start = (bf16[3,3,128,256]{3,2,1,0:T(8,128)(2,1)S(1)}, bf16[3,3,128,256]{3,2,1,0:T(8,128)(2,1)}, u32[]{:S(2)}) copy-start(bf16[3,3,128,256]{3,2,1,0:T(8,128)(2,1)} %in_w.1) | copy-start | bytes 1769476
  1.7 1.1 %copy-start.1 = (bf16[3,3,256,128]{3,2,1,0:T(8,128)(2,1)S(1)}, bf16[3,3,256,128]{3,2,1,0:T(8,128)(2,1)}, u32[]{:S(2)}) copy-start(bf16[3,3,256,128]{3,2,1,0:T(8,128)(2,1)} %out_w.1) | copy-start | bytes 1769476
  2.8 0.9 %copy-start.2 = (bf16[1,8,64,128]{3,2,1,0:T(8,128)(2,1)S(1)}, bf16[1,8,64,128]{3,2,1,0:T(8,128)(2,1)}, u32[]{:S(2)}) copy-start(bf16[1,8,64,128]{3,2,1,0:T(8,128)(2,1)} %frames.1) | copy-start | bytes 393220
  3.7 0.9 %copy-start.3 = (bf16[1,8,64,128]{3,2,1,0:T(8,128)(2,1)S(1)}, bf16[1,8,64,128]{3,2,1,0:T(8,128)(2,1)}, u32[]{:S(2)}) copy-start(bf16[1,8,64,128]{3,2,1,0:T(8,128)(2,1)} %cot.1) | copy-start | bytes 393220
  4.6 0.7 copy-start.4
  5.3 0.7 copy-start.5
